TPU v7x, 256 devices: a whole 4x4x8 slice. The times are simulated.
256 devices in a mesh: shock: 32 (over z, x), trans: 8 (over y, core).
Axes of the slice: x: 4, y: 4, z: 8, core: 2. Of those that a mesh axis runs over, the one named last changes fastest.
Arguments:
- conserved: float32 [11, 10, 524288], P(None, None, ('shock', 'trans')), may hold values from -6 to 6
- cell_size: float32 [524288], P(('shock', 'trans')), may hold values from 0.5 to 2
- sound_speed: float32 [524288], P(('shock', 'trans')), may hold values from 0.3 to 1.8
- jacobian: float32 [3, 11, 11], replicated, may hold values from -1.75 to 1.75
- derivative: float32 [3, 10, 10], replicated, may hold values from -2 to 2
- restriction: float32 [4, 6, 10], replicated, may hold values from -2 to 2
- lifting: float32 [4, 10, 6], replicated, may hold values from -2.5 to 2.5
- vertex_velocity: float32 [3, 131072], P(None, ('shock', 'trans')), may hold values from -1.8 to 1.8
- share_index: int32 [2, 32768], P(None, ('shock', 'trans')), may hold values from 0 to 511
- elem_vertex: int32 [4, 524288], P(None, ('shock', 'trans')), may hold values from 0 to 767
- inner_elem: int32 [2, 1048576], P(None, ('shock', 'trans')), may hold values from 0 to 2047
- inner_face: int32 [2, 1048576], P(None, ('shock', 'trans')), may hold values from 0 to 3
- inner_normal: float32 [3, 1048576], P(None, ('shock', 'trans')), may hold values from -3 to 3
- slab_elem: int32 [2, 65536], P(None, ('shock', 'trans')), may hold values from 0 to 2047
- slab_face: int32 [2, 65536], P(None, ('shock', 'trans')), may hold values from 0 to 3
- slab_normal: float32 [3, 2, 65536], P(None, None, ('shock', 'trans')), may hold values from -3 to 3
- peer_elem: int32 [8, 16384], P(None, ('shock', 'trans')), may hold values from 0 to 2047
- peer_face: int32 [8, 16384], P(None, ('shock', 'trans')), may hold values from 0 to 3
- peer_normal: float32 [3, 8, 16384], P(None, None, ('shock', 'trans')), may hold values from -3 to 3
- peer_count: int32 [8, 256], P(None, ('shock', 'trans')), may hold values from 0 to 64, as said below
Outputs:
- rate: float32 [11, 10, 524288], P(None, None, ('shock', 'trans'))
- step_size: float32 [], replicated
Inputs may be any that keep to these rules, and one draw needn't show every extreme that they name: peer_count[q, p] is the same for partition p at trans position q' and the partition of the same slab at position q when read from the other side, is 0 for q equal to p's own position, and equals 64 for some pair of each slab; slots at or past it are padding.
All inputs are finite; a program needn't handle non-finite values.
Results may differ from a plain program's by a relative error of at most 0.0003.
Values sent between devices are 32-bit elements; how exact they have to be, the bound alone decides.
No kernel may reach another device: no remote copies, remote signals or barrier semaphores. Data moves between devices by JAX's collectives and lax.ppermute only.
A program may use at most 128 MiB of HBM per device.

v0:
```python
import functools

import jax
import jax.numpy as jnp
import numpy as np
from jax import lax
from jax.experimental import pallas as pl
from jax.experimental.pallas import tpu as pltpu
from jax.sharding import PartitionSpec as P

HIGHEST_PREC = lax.Precision.HIGHEST
CFL_NUMBER = 0.3
BF16 = jnp.bfloat16
F32 = jnp.float32

VARS = 11
BASIS = 10
FACE = 6
ROWS = 112
TROWS = 72
ELEM_BLOCK = 256
TILE = 256
CHUNK = 512


def expansion_tables():
    rows = np.arange(ROWS)
    outer = np.zeros((ROWS, 16), np.float32)
    inner = np.zeros((ROWS, 16), np.float32)
    live = rows < VARS * BASIS
    outer[rows[live], rows[live] // VARS] = 1.0
    inner[rows[live], rows[live] % VARS] = 1.0
    face_live = (np.arange(TROWS) < VARS * FACE).astype(np.float32)[:, None]
    outer_face = outer[:TROWS] * face_live
    inner_face = inner[:TROWS] * face_live
    outer3 = np.tile(outer.T, (1, 3))
    inner3 = np.tile(inner.T, (1, 3))
    outer_face3 = np.tile(outer_face.T, (1, 3))
    inner_face3 = np.tile(inner_face.T, (1, 3))
    bound = np.zeros((TROWS, 3 * ROWS), np.float32)
    bound[VARS * FACE, VARS * BASIS :: ROWS] = 1.0
    return (outer, inner, outer_face, inner_face, outer3, inner3, outer_face3, inner_face3, bound)


def exact_dot(left, right):
    return jnp.dot(left, right, precision=HIGHEST_PREC, preferred_element_type=F32)


def split3_cols(wide):
    third = wide.shape[1] // 3
    high = wide.astype(BF16).astype(F32)
    lane = lax.broadcasted_iota(jnp.int32, wide.shape, 1)
    return jnp.where(lane < 2 * third, high, wide - high).astype(BF16)


def weights_kernel(
    jac, der, res, lif, outer, inner, outer_face, inner_face, outer3, inner3, outer_face3,
    inner_face3, bound, w_elem, w_trace, w_flux, w_lift,
):
    same_var = exact_dot(inner[...], inner3[...])
    total = None
    for d in range(3):
        der_wide = exact_dot(outer[...], exact_dot(der[d], outer3[...]))
        jac_wide = exact_dot(inner[...], exact_dot(jac[d], inner3[...]))
        term = der_wide * jac_wide
        total = term if total is None else total + term
        w_elem[(d + 1) * ROWS : (d + 2) * ROWS, :] = split3_cols(der_wide * same_var)
        same_basis = exact_dot(outer_face[...], outer_face3[...])
        jac_face = exact_dot(inner_face[...], exact_dot(jac[d], inner_face3[...]))
        w_flux[d * TROWS : (d + 1) * TROWS, :] = split3_cols(jac_face * same_basis)
    w_elem[0:ROWS, :] = split3_cols(total)
    same_var_in = exact_dot(inner_face[...], inner3[...])
    same_var_out = exact_dot(inner[...], inner_face3[...])
    for k in range(4):
        res_wide = exact_dot(outer_face[...], exact_dot(res[k], outer3[...]))
        w_trace[k * TROWS : (k + 1) * TROWS, :] = split3_cols(res_wide * same_var_in + bound[...])
        lif_wide = exact_dot(outer[...], exact_dot(lif[k], outer_face3[...]))
        w_lift[k * ROWS : (k + 1) * ROWS, :] = split3_cols(lif_wide * same_var_out)


def make_weights(jacobian, derivative, restriction, lifting):
    tables = [jnp.asarray(table) for table in expansion_tables()]
    padded = [
        jnp.pad(value, ((0, 0), (0, 16 - value.shape[1]), (0, 16 - value.shape[2])))
        for value in (jacobian, derivative, restriction, lifting)
    ]
    return pl.pallas_call(
        weights_kernel,
        out_shape=(
            jax.ShapeDtypeStruct((4 * ROWS, 3 * ROWS), BF16),
            jax.ShapeDtypeStruct((4 * TROWS, 3 * ROWS), BF16),
            jax.ShapeDtypeStruct((3 * TROWS, 3 * TROWS), BF16),
            jax.ShapeDtypeStruct((4 * ROWS, 3 * TROWS), BF16),
        ),
        name="weights",
    )(*padded, *tables)


def lane_gather(table, tiles, index_row):
    wide = jnp.broadcast_to(index_row, (8, 128))
    low = wide & 127
    high = lax.shift_right_logical(wide, 7)
    picked = jnp.take_along_axis(table[:, 0:128], low, axis=1)
    for t in range(1, tiles):
        other = jnp.take_along_axis(table[:, t * 128 : (t + 1) * 128], low, axis=1)
        picked = jnp.where(high == t, other, picked)
    return picked


def share_kernel(velocity, share, to_lower, to_upper, table):
    table[...] = jnp.zeros_like(table)
    table[0:3, :] = velocity[...]
    tiles = velocity.shape[1] // 128
    to_lower[...] = lane_gather(table, tiles, share[0:1, :])
    to_upper[...] = lane_gather(table, tiles, share[1:2, :])


def mesh_kernel(velocity, from_lower, from_upper, corners, sizes, sounds, geom, least, table):
    own = velocity.shape[1]
    table[...] = jnp.zeros_like(table)
    table[0:3, 0:own] = velocity[...]
    table[:, own : own + 128] = from_lower[...]
    table[:, own + 128 : own + 256] = from_upper[...]
    tiles = (own + 256) // 128
    elems = corners.shape[1]
    for j in range(elems // 128):
        cols = slice(j * 128, (j + 1) * 128)
        total = None
        for corner in range(4):
            value = lane_gather(table, tiles, corners[corner : corner + 1, cols])
            total = value if total is None else total + value
        geom[:, cols] = total * 0.25
    moves = jnp.abs(geom[0:3, :])
    bound = sounds[...] + moves[0:1] + moves[1:2] + moves[2:3]
    geom[3:4, :] = bound
    geom[4:5, :] = 1.0 / sizes[...]
    least[...] = jnp.broadcast_to(
        jnp.min(sizes[...] / bound, axis=1, keepdims=True), least.shape
    )


def split3_rows(value):
    high = value.astype(BF16)
    low = (value - high.astype(F32)).astype(BF16)
    return jnp.concatenate([high, low, high], axis=0)


def split2_rows(value):
    high = value.astype(BF16)
    low = (value - high.astype(F32)).astype(BF16)
    return jnp.concatenate([high, low], axis=0)


def fields_kernel(state, geom, w_elem, c_out, l1_out, l2_out, l3_out, table):
    for b in range(BASIS):
        c_out[b * VARS : (b + 1) * VARS, :] = state[b]
    c_out[BASIS * VARS : BASIS * VARS + 1, :] = geom[3:4, :]
    c_out[BASIS * VARS + 1 : ROWS, :] = jnp.zeros((1, c_out.shape[1]), F32)
    value = c_out[...]
    for i, out in enumerate((l1_out, l2_out, l3_out)):
        pieces = split3_rows(value)
        table[2 * ROWS * i : 2 * ROWS * (i + 1), :] = pieces[0 : 2 * ROWS]
        parts = jnp.dot(w_elem[...], pieces, preferred_element_type=F32)
        value = (
            parts[0:ROWS]
            - geom[0:1, :] * parts[ROWS : 2 * ROWS]
            - geom[1:2, :] * parts[2 * ROWS : 3 * ROWS]
            - geom[2:3, :] * parts[3 * ROWS : 4 * ROWS]
        ) * geom[4:5, :]
        out[...] = value


def make_fields(state, geom, w_elem):
    elems = geom.shape[1]
    full = jax.ShapeDtypeStruct((ROWS, elems), F32)
    block = pl.BlockSpec((ROWS, CHUNK), lambda i: (0, i))
    return pl.pallas_call(
        fields_kernel,
        grid=(elems // CHUNK,),
        in_specs=[
            pl.BlockSpec((BASIS, VARS, CHUNK), lambda i: (0, 0, i)),
            pl.BlockSpec((8, CHUNK), lambda i: (0, i)),
            pl.BlockSpec((4 * ROWS, 3 * ROWS), lambda i: (0, 0)),
        ],
        out_specs=[block] * 4 + [pl.BlockSpec((6 * ROWS, CHUNK), lambda i: (0, i))],
        out_shape=[full] * 4 + [jax.ShapeDtypeStruct((6 * ROWS, elems), BF16)],
        name="fields",
    )(state, geom, w_elem)


def build_selection(index_row, select):
    count = index_row.shape[1]
    low = index_row & (ELEM_BLOCK - 1)
    high = lax.shift_right_logical(index_row, 8)
    place = lax.broadcasted_iota(jnp.int32, (ELEM_BLOCK, count), 0)
    match = jnp.where(place == low, 1.0, 0.0).astype(BF16)
    for t in range(select.shape[0] // ELEM_BLOCK):
        here = jnp.where(high == t, 1.0, 0.0).astype(BF16)
        select[t * ELEM_BLOCK : (t + 1) * ELEM_BLOCK, :] = match * here


def choose(stacked, which, rows):
    value = stacked[0:rows]
    for k in range(1, 4):
        value = jnp.where(which == k, stacked[k * rows : (k + 1) * rows], value)
    return value


def traces_of(picked, which, w_trace):
    pieces = jnp.concatenate([picked, picked[0:ROWS]], axis=0)
    stacked = jnp.dot(w_trace[...], pieces, preferred_element_type=F32)
    return choose(stacked, which, TROWS)


def border_kernel(elem, face, table, w_trace, own, to_lower, to_upper, to_peer, select):
    step = pl.program_id(0)
    build_selection(elem[...], select)
    picked = jnp.dot(table[...], select[...], preferred_element_type=F32).astype(BF16)
    which = face[...]
    own[3 * TROWS :, :] = jnp.zeros((8, own.shape[1]), F32)
    for i in range(3):
        own[i * TROWS : (i + 1) * TROWS, :] = traces_of(
            picked[2 * ROWS * i : 2 * ROWS * (i + 1)], which, w_trace
        )

    @pl.when(step == 0)
    def _():
        to_lower[...] = own[0 : 3 * TROWS, 0:256]
        to_upper[...] = own[0 : 3 * TROWS, 256:512]

    @pl.when(step == 1)
    def _():
        left = lax.broadcasted_iota(jnp.int32, (ROWS, 128), 1) < 64
        for m in range(4):
            top = own[0:ROWS, m * 128 : (m + 1) * 128]
            bottom = own[ROWS : 2 * ROWS, m * 128 : (m + 1) * 128]
            to_peer[2 * m] = jnp.where(left, top, pltpu.roll(bottom, 64, 1))
            to_peer[2 * m + 1] = jnp.where(left, pltpu.roll(top, 64, 1), bottom)


def make_border(elem, face, table, w_trace):
    elems = table.shape[1]
    return pl.pallas_call(
        border_kernel,
        grid=(2,),
        in_specs=[
            pl.BlockSpec((1, 512), lambda i: (0, i)),
            pl.BlockSpec((1, 512), lambda i: (0, i)),
            pl.BlockSpec((6 * ROWS, elems), lambda i: (0, 0)),
            pl.BlockSpec((4 * TROWS, 3 * ROWS), lambda i: (0, 0)),
        ],
        out_specs=[
            pl.BlockSpec((2 * ROWS, 512), lambda i: (0, i)),
            pl.BlockSpec((3 * TROWS, 256), lambda i: (0, 0)),
            pl.BlockSpec((3 * TROWS, 256), lambda i: (0, 0)),
            pl.BlockSpec((8, ROWS, 128), lambda i: (0, 0, 0)),
        ],
        out_shape=[
            jax.ShapeDtypeStruct((2 * ROWS, 1024), F32),
            jax.ShapeDtypeStruct((3 * TROWS, 256), F32),
            jax.ShapeDtypeStruct((3 * TROWS, 256), F32),
            jax.ShapeDtypeStruct((8, ROWS, 128), F32),
        ],
        scratch_shapes=[pltpu.VMEM((elems, 512), BF16)],
        name="border",
    )(elem, face, table, w_trace)


def flux_parts(own, theirs, normal, w_flux):
    jump = theirs - own
    bound = jnp.maximum(own[66:67], theirs[66:67])
    parts = jnp.dot(w_flux[...], split3_rows(jump), preferred_element_type=F32)
    central = (
        normal[0:1] * parts[0:TROWS]
        + normal[1:2] * parts[TROWS : 2 * TROWS]
        + normal[2:3] * parts[2 * TROWS : 3 * TROWS]
    )
    return central, bound * jump


def lift_and_add(values, which, w_lift, select, total):
    stacked = jnp.dot(w_lift[...], split3_rows(values), preferred_element_type=F32)
    pieces = split2_rows(choose(stacked, which, ROWS))
    total[...] += lax.dot_general(
        pieces, select[...], (((1,), (1,)), ((), ())), preferred_element_type=F32
    )


def combine(first, second, third, half, sixth):
    return first + half * second + sixth * third


def rate_kernel(
    step_ref, c_ref, l1_ref, l2_ref, l3_ref, geom, own, from_lower, from_upper, from_peer, b_elem,
    b_face, b_normal, b_live, elem, face, normal, w_trace, w_flux, w_lift, out, table, total,
    select, theirs,
):
    step = pl.program_id(0)
    tau = step_ref[0, 0]
    half = -0.5 * tau
    sixth = tau * tau / 6.0

    @pl.when(step == 0)
    def _():
        total[...] = jnp.zeros_like(total)
        for j in range(c_ref.shape[1] // CHUNK):
            cols = slice(j * CHUNK, (j + 1) * CHUNK)
            table[:, cols] = split2_rows(
                combine(c_ref[:, cols], l1_ref[:, cols], l2_ref[:, cols], half, sixth)
            )
        left = lax.broadcasted_iota(jnp.int32, (ROWS, 128), 1) < 64
        theirs[0 : 3 * TROWS, 0:256] = from_lower[...]
        theirs[0 : 3 * TROWS, 256:512] = from_upper[...]
        for m in range(4):
            cols = slice(512 + m * 128, 512 + (m + 1) * 128)
            one, two = from_peer[2 * m], from_peer[2 * m + 1]
            theirs[0:ROWS, cols] = jnp.where(left, one, pltpu.roll(two, 64, 1))
            theirs[ROWS : 2 * ROWS, cols] = jnp.where(left, pltpu.roll(one, 64, 1), two)
        for j in range(2):
            cols = slice(j * 512, (j + 1) * 512)
            build_selection(b_elem[:, cols], select)

            def merged(ref):
                return combine(
                    ref[0:TROWS, cols],
                    ref[TROWS : 2 * TROWS, cols],
                    ref[2 * TROWS : 3 * TROWS, cols],
                    half,
                    sixth,
                )

            central, upwind = flux_parts(merged(own), merged(theirs), b_normal[:, cols], w_flux)
            values = (0.5 * (central - upwind)) * b_live[:, cols]
            lift_and_add(values, b_face[:, cols], w_lift, select, total)

    index_row = jnp.concatenate([elem[0:1, :], elem[1:2, :]], axis=1)
    which = jnp.concatenate([face[0:1, :], face[1:2, :]], axis=1)
    build_selection(index_row, select)
    picked = jnp.dot(table[...], select[...], preferred_element_type=F32).astype(BF16)
    traces = traces_of(picked, which, w_trace)
    central, upwind = flux_parts(traces[:, 0:TILE], traces[:, TILE:], normal[...], w_flux)
    values = jnp.concatenate([0.5 * (central - upwind), 0.5 * (central + upwind)], axis=1)
    lift_and_add(values, which, w_lift, select, total)

    @pl.when(step == pl.num_programs(0) - 1)
    def _():
        for j in range(c_ref.shape[1] // CHUNK):
            cols = slice(j * CHUNK, (j + 1) * CHUNK)
            lifted = total[0:ROWS, cols] + total[ROWS : 2 * ROWS, cols]
            volume = combine(l1_ref[:, cols], l2_ref[:, cols], l3_ref[:, cols], half, sixth)
            rate = -(volume + lifted * geom[4:5, cols])
            for b in range(BASIS):
                out[b, :, cols] = rate[b * VARS : (b + 1) * VARS]


def make_rate(step_size, fields, geom, own, received, border, inner, weights):
    elems = geom.shape[1]
    faces = inner[0].shape[1]
    whole = pl.BlockSpec(memory_space=pltpu.VMEM)
    tiled = lambda rows: pl.BlockSpec((rows, TILE), lambda i: (0, i))
    return pl.pallas_call(
        rate_kernel,
        grid=(faces // TILE,),
        in_specs=[pl.BlockSpec(memory_space=pltpu.SMEM)]
        + [whole] * 13
        + [tiled(2), tiled(2), tiled(3)]
        + [whole] * 3,
        out_specs=whole,
        out_shape=jax.ShapeDtypeStruct((BASIS, VARS, elems), F32),
        scratch_shapes=[
            pltpu.VMEM((2 * ROWS, elems), BF16),
            pltpu.VMEM((2 * ROWS, elems), F32),
            pltpu.VMEM((elems, 2 * TILE), BF16),
            pltpu.VMEM((2 * ROWS, 1024), F32),
        ],
        name="rate",
    )(step_size, *fields, geom, own, *received, *border, *inner, *weights)


def body(
    conserved,
    cell_size,
    sound_speed,
    jacobian,
    derivative,
    restriction,
    lifting,
    vertex_velocity,
    share_index,
    elem_vertex,
    inner_elem,
    inner_face,
    inner_normal,
    slab_elem,
    slab_face,
    slab_normal,
    peer_elem,
    peer_face,
    peer_normal,
    peer_count,
):
    elems = conserved.shape[2]
    slabs = lax.axis_size("shock")
    devices = slabs * lax.axis_size("trans")
    up = [(i, i + 1) for i in range(slabs - 1)]
    down = [(i + 1, i) for i in range(slabs - 1)]

    shared = jax.ShapeDtypeStruct((8, 128), F32)
    to_lower, to_upper = pl.pallas_call(
        share_kernel,
        out_shape=(shared, shared),
        scratch_shapes=[pltpu.VMEM((8, vertex_velocity.shape[1]), F32)],
        name="share",
    )(vertex_velocity, share_index)
    from_lower = lax.ppermute(to_upper, "shock", up)
    from_upper = lax.ppermute(to_lower, "shock", down)
    w_elem, w_trace, w_flux, w_lift = make_weights(jacobian, derivative, restriction, lifting)
    geom, least = pl.pallas_call(
        mesh_kernel,
        out_shape=(
            jax.ShapeDtypeStruct((8, elems), F32),
            jax.ShapeDtypeStruct((1, devices), F32),
        ),
        scratch_shapes=[pltpu.VMEM((8, vertex_velocity.shape[1] + 256), F32)],
        name="mesh",
    )(
        vertex_velocity,
        from_lower,
        from_upper,
        elem_vertex,
        cell_size.reshape(1, elems),
        sound_speed.reshape(1, elems),
    )
    all_least = lax.all_to_all(
        least.reshape(devices), ("shock", "trans"), split_axis=0, concat_axis=0, tiled=True
    )

    state = jnp.transpose(conserved, (1, 0, 2))
    *fields, table = make_fields(state, geom, w_elem)
    live = (jnp.arange(peer_elem.shape[1])[None, :] < peer_count).astype(F32)
    b_elem = jnp.concatenate([slab_elem.reshape(1, -1), peer_elem.reshape(1, -1)], axis=1)
    b_face = jnp.concatenate([slab_face.reshape(1, -1), peer_face.reshape(1, -1)], axis=1)
    b_normal = jnp.concatenate([slab_normal.reshape(3, -1), peer_normal.reshape(3, -1)], axis=1)
    b_live = jnp.concatenate([jnp.ones((1, slab_elem.size), F32), live.reshape(1, -1)], axis=1)
    own, slab_down, slab_up, peer_send = make_border(b_elem, b_face, table, w_trace)
    slab_lower = lax.ppermute(slab_up, "shock", up)
    slab_upper = lax.ppermute(slab_down, "shock", down)
    peer_recv = lax.all_to_all(peer_send, "trans", split_axis=0, concat_axis=0, tiled=True)

    step_size = CFL_NUMBER * jnp.min(all_least)
    rate = make_rate(
        step_size.reshape(1, 1),
        fields,
        geom,
        own,
        (slab_lower, slab_upper, peer_recv),
        (b_elem, b_face, b_normal, b_live),
        (inner_elem, inner_face, inner_normal),
        (w_trace, w_flux, w_lift),
    )
    return (jnp.transpose(rate, (1, 0, 2)), step_size)


def solution(mesh):
    return jax.shard_map(
        body,
        mesh=mesh,
        in_specs=(
            P(None, None, ("shock", "trans")),
            P(("shock", "trans")),
            P(("shock", "trans")),
            P(),
            P(),
            P(),
            P(),
            P(None, ("shock", "trans")),
            P(None, ("shock", "trans")),
            P(None, ("shock", "trans")),
            P(None, ("shock", "trans")),
            P(None, ("shock", "trans")),
            P(None, ("shock", "trans")),
            P(None, ("shock", "trans")),
            P(None, ("shock", "trans")),
            P(None, None, ("shock", "trans")),
            P(None, ("shock", "trans")),
            P(None, ("shock", "trans")),
            P(None, None, ("shock", "trans")),
            P(None, ("shock", "trans")),
        ),
        out_specs=(P(None, None, ("shock", "trans")), P()),
        check_vma=False,
    )
```

profile of v0, /device:TPU:110, one launch (start us, length us, event | category | flops | bytes accessed | tf_op | source)
XLA Modules:
  0.0 126.2 jit_solution(9072598639602504948)
XLA Ops:
  0.6 1.4 %share.2 = (f32[8,128]{1,0:T(8,128)}, f32[8,128]{1,0:T(8,128)}) custom-call(f32[3,512]{1,0:T(4,128)} %velocity.3, s32[2,128]{1,0:T(2,128)} %share.3), custom_call_target="tpu_custom_call" | custom-call | tf_op jit(solution)/shard_map/share/pallas_call | solution.py:409
  2.0 4.9 %collective-permute-start = (f32[8,128]{1,0:T(8,128)}, f32[8,128]{1,0:T(8,128)S(1)}, u32[]{:S(2)}, u32[]{:S(2)}) collective-permute-start(f32[8,128]{1,0:T(8,128)} %get-tuple-element.19), channel_id=1, source_target_pairs={{0,8},{8,16},{16,24},{24,32},{32,40},{40,48},{48,56},{56,64},{64,7... | collective-permute-start | bytes 12296 | tf_op jit(solution)/shard_map/ppermute | solution.py:415
  7.0 1.9 %collective-permute-start.1 = (f32[8,128]{1,0:T(8,128)}, f32[8,128]{1,0:T(8,128)S(1)}, u32[]{:S(2)}, u32[]{:S(2)}) collective-permute-start(f32[8,128]{1,0:T(8,128)} %get-tuple-element.20), channel_id=1, source_target_pairs={{8,0},{16,8},{24,16},{32,24},{40,32},{48,40},{56,48},{64,56},{72,6... | collective-permute-start | bytes 12296 | tf_op jit(solution)/shard_map/ppermute | solution.py:416
  8.9 0.7 copy.44
  9.6 0.7 copy.45
  10.3 0.8 reshape.67
  11.0 0.8 reshape.69
  11.8 0.0 collective-permute-done.from_lower
  11.8 4.2 %collective-permute-done.1.from_upper = f32[8,128]{1,0:T(8,128)S(1)} collective-permute-done((f32[8,128]{1,0:T(8,128)}, f32[8,128]{1,0:T(8,128)S(1)}, u32[]{:S(2)}, u32[]{:S(2)}) %collective-permute-start.1) | collective-permute-done | bytes 4128 | tf_op jit(solution)/shard_map/ppermute | solution.py:416
  16.0 0.0 copy-done.5
  16.0 0.6 copy-done.6
  16.6 2.2 %mesh.1 = (f32[8,2048]{1,0:T(8,128)}, f32[1,256]{1,0:T(1,128)}) custom-call(f32[3,512]{1,0:T(4,128)} %velocity.3, f32[8,128]{1,0:T(8,128)} %copy-done.5, f32[8,128]{1,0:T(8,128)} %copy-done.6, s32[4,2048]{1,0:T(4,128)} %corners.1, f32[1,2048]{1,0:T(1,128)} %bitcast.20, f32[1,2048]{1,0:T(1,128)} %bitcast.21), custom_call_target="tpu_custom_call" | custom-call | tf_op jit(solution)/shard_map/mesh/pallas_call | solution.py:418
  18.8 1.5 %copy.39 = f32[256,1,1]{2,1,0:T(1,128)} copy(f32[256,1,1]{0,2,1:T(1,128)} %bitcast.25) | data formatting | bytes 2048 | tf_op jit(solution)/shard_map/all_to_all | solution.py:434
  20.2 11.1 %all-to-all-start = ((f32[256,1,1]{2,1,0:T(1,128)}), f32[256,1,1]{2,1,0:T(1,128)S(1)}, u32[]{:S(2)}, u32[]{:S(2)}) async-start(f32[256,1,1]{2,1,0:T(1,128)} %copy.39), calls=%async_computation | async-start | bytes 262144 | tf_op jit(solution)/shard_map/all_to_all | solution.py:434
  31.3 0.0 copy-start.3
  31.4 0.0 copy-start.4
  31.4 0.7 copy.40
  32.1 0.7 copy.41
  32.8 0.6 pad.18.jac
  33.4 0.6 pad.19.der
  34.0 0.7 copy.42
  34.8 0.6 pad.20.res
  35.4 0.8 copy.43
  36.2 0.6 pad.21.lif
  36.8 0.8 reshape.71
  37.6 0.7 copy.46
  38.3 6.3 %weights.1 = (bf16[448,336]{1,0:T(8,128)(2,1)}, bf16[288,336]{1,0:T(8,128)(2,1)}, bf16[216,216]{1,0:T(8,128)(2,1)}, bf16[448,216]{1,0:T(8,128)(2,1)}) custom-call(f32[3,16,16]{2,1,0:T(8,128)} %pad.18.jac, f32[3,16,16]{2,1,0:T(8,128)} %pad.19.der, f32[4,16,16]{2,1,0:T(8,128)} %pad.20.res, f32[4,16,16]{2,1,0:T(8,128)} %pad.21.lif, ...), custom_call_target="tpu_custom_call" | custom-call | tf_op jit(solution)/shard_map/weights/pallas_call | solution.py:87
  44.6 7.2 %fields.1 = (f32[112,2048]{1,0:T(8,128)}, f32[112,2048]{1,0:T(8,128)}, f32[112,2048]{1,0:T(8,128)}, f32[112,2048]{1,0:T(8,128)}, bf16[672,2048]{1,0:T(8,128)(2,1)}) custom-call(f32[10,11,2048]{2,1,0:T(8,128)} %bitcast.15, f32[8,2048]{1,0:T(8,128)} %get-tuple-element.22.geom, bf16[448,336]{1,0:T(8,128)(2,1)} %get-tuple-element.23.w_elem), custom_call_target="tpu_custom_call" | custom-call | tf_op jit(solution)/shard_map/fields/pallas_call | solution.py:177
  51.7 0.0 copy-done.3
  51.7 0.0 copy-done.4
  51.8 0.0 copy-start.7
  51.8 7.3 %border.1 = (f32[224,1024]{1,0:T(8,128)}, f32[216,256]{1,0:T(8,128)}, f32[216,256]{1,0:T(8,128)}, f32[8,112,128]{2,1,0:T(8,128)}) custom-call(s32[1,1024]{1,0:T(1,128)} %copy-done.3, s32[1,1024]{1,0:T(1,128)} %copy-done.4, bf16[672,2048]{1,0:T(8,128)(2,1)} %get-tuple-element.28.table, bf16[288,336]{1,0:T(8,128)(2,1)} %get-tuple-element.29.w_trace), custom_call_target="tpu_custom_call" | custom-call | tf_op jit(solution)/shard_map/border/pallas_call | solution.py:243
  59.0 0.0 all-to-all-done
  59.1 4.9 %all-to-all-start.1 = ((f32[8,112,128]{2,1,0:T(8,128)}), f32[8,112,128]{2,1,0:T(8,128)S(1)}, u32[]{:S(2)}, u32[]{:S(2)}) async-start(f32[8,112,128]{2,1,0:T(8,128)} %get-tuple-element.33), calls=%async_computation.1 | async-start | bytes 917504 | tf_op jit(solution)/shard_map/all_to_all | solution.py:448
  63.9 0.0 copy-done.7
  63.9 0.1 iota_compare_fusion
  64.0 0.1 convert_element_type.19
  64.1 4.8 %collective-permute-start.2 = (f32[216,256]{1,0:T(8,128)}, f32[216,256]{1,0:T(8,128)S(1)}, u32[]{:S(2)}, u32[]{:S(2)}) collective-permute-start(f32[216,256]{1,0:T(8,128)} %get-tuple-element.31), channel_id=1, source_target_pairs={{0,8},{8,16},{16,24},{24,32},{32,40},{40,48},{48,56},{56,64},{64,7... | collective-permute-start | bytes 663560 | tf_op jit(solution)/shard_map/ppermute | solution.py:446
  68.9 2.1 %collective-permute-start.3 = (f32[216,256]{1,0:T(8,128)}, f32[216,256]{1,0:T(8,128)S(1)}, u32[]{:S(2)}, u32[]{:S(2)}) collective-permute-start(f32[216,256]{1,0:T(8,128)} %get-tuple-element.32), channel_id=1, source_target_pairs={{8,0},{16,8},{24,16},{32,24},{40,32},{48,40},{56,48},{64,56},{72,6... | collective-permute-start | bytes 663560 | tf_op jit(solution)/shard_map/ppermute | solution.py:447
  71.0 0.6 pad_convert_fusion.b_live
  71.6 0.6 pad_maximum_fusion.b_normal
  72.2 0.9 reduce_min.9
  73.7 0.4 collective-permute-done.2.from_lower
  74.2 7.3 %collective-permute-done.3.from_upper = f32[216,256]{1,0:T(8,128)S(1)} collective-permute-done((f32[216,256]{1,0:T(8,128)}, f32[216,256]{1,0:T(8,128)S(1)}, u32[]{:S(2)}, u32[]{:S(2)}) %collective-permute-start.3) | collective-permute-done | bytes 221216 | tf_op jit(solution)/shard_map/ppermute | solution.py:447
  81.5 0.0 all-to-all-done.1.from_peer
  81.5 0.7 copy-done.2
  82.2 0.2 copy-done
  82.3 42.7 %rate.1 = f32[10,11,2048]{2,1,0:T(8,128)} custom-call(f32[1,1]{1,0:T(1,128)} %bitcast.3.step_ref, f32[112,2048]{1,0:T(8,128)} %get-tuple-element.24.c_ref, f32[112,2048]{1,0:T(8,128)} %get-tuple-element.25.l1_ref, f32[112,2048]{1,0:T(8,128)} %get-tuple-element.26.l2_ref, f32[112,2048]{1,0:T(8,128)} %get-tuple-element.27.l3_ref, ...), custom_call_target="tpu_custom_call" | custom-call | tf_op jit(solution)/shard_map/rate/pallas_call | solution.py:361
  (9 shorter events, 0.0 us)
Async XLA Ops:
  2.0 9.8 %collective-permute-start = (f32[8,128]{1,0:T(8,128)}, f32[8,128]{1,0:T(8,128)S(1)}, u32[]{:S(2)}, u32[]{:S(2)}) collective-permute-start(f32[8,128]{1,0:T(8,128)} %get-tuple-element.19), channel_id=1, source_target_pairs={{0,8},{8,16},{16,24},{24,32},{32,40},{40,48},{48,56},{56,64},{64,7... | collective-permute-start | bytes 12296 | tf_op jit(solution)/shard_map/ppermute | solution.py:415
  7.0 9.0 %collective-permute-start.1 = (f32[8,128]{1,0:T(8,128)}, f32[8,128]{1,0:T(8,128)S(1)}, u32[]{:S(2)}, u32[]{:S(2)}) collective-permute-start(f32[8,128]{1,0:T(8,128)} %get-tuple-element.20), channel_id=1, source_target_pairs={{8,0},{16,8},{24,16},{32,24},{40,32},{48,40},{56,48},{64,56},{72,6... | collective-permute-start | bytes 12296 | tf_op jit(solution)/shard_map/ppermute | solution.py:416
  11.8 4.2 %copy-start.5 = (f32[8,128]{1,0:T(8,128)}, f32[8,128]{1,0:T(8,128)S(1)}, u32[]{:S(2)}) copy-start(f32[8,128]{1,0:T(8,128)S(1)} %collective-permute-done.from_lower) | copy-start | bytes 12292
  16.0 0.6 copy-start.6
  20.2 38.8 %all-to-all-start = ((f32[256,1,1]{2,1,0:T(1,128)}), f32[256,1,1]{2,1,0:T(1,128)S(1)}, u32[]{:S(2)}, u32[]{:S(2)}) async-start(f32[256,1,1]{2,1,0:T(1,128)} %copy.39), calls=%async_computation | async-start | bytes 262144 | tf_op jit(solution)/shard_map/all_to_all | solution.py:434
  31.3 20.4 %copy-start.3 = (s32[1,1024]{1,0:T(1,128)}, s32[1,1024]{1,0:T(1,128)S(1)}, u32[]{:S(2)}) copy-start(s32[1,1024]{1,0:T(1,128)S(1)} %get-tuple-element.36.elem.b_elem) | copy-start | bytes 12292
  31.4 20.4 %copy-start.4 = (s32[1,1024]{1,0:T(1,128)}, s32[1,1024]{1,0:T(1,128)S(1)}, u32[]{:S(2)}) copy-start(s32[1,1024]{1,0:T(1,128)S(1)} %get-tuple-element.37.face.b_face) | copy-start | bytes 12292
  51.8 12.2 %copy-start.7 = (s32[8,1]{0,1:T(1,128)S(1)}, s32[8,1]{0,1:T(1,128)}, u32[]{:S(2)}) copy-start(s32[8,1]{0,1:T(1,128)} %param.48) | copy-start | bytes 100
  59.1 22.4 %all-to-all-start.1 = ((f32[8,112,128]{2,1,0:T(8,128)}), f32[8,112,128]{2,1,0:T(8,128)S(1)}, u32[]{:S(2)}, u32[]{:S(2)}) async-start(f32[8,112,128]{2,1,0:T(8,128)} %get-tuple-element.33), calls=%async_computation.1 | async-start | bytes 917504 | tf_op jit(solution)/shard_map/all_to_all | solution.py:448
  64.1 10.1 %collective-permute-start.2 = (f32[216,256]{1,0:T(8,128)}, f32[216,256]{1,0:T(8,128)S(1)}, u32[]{:S(2)}, u32[]{:S(2)}) collective-permute-start(f32[216,256]{1,0:T(8,128)} %get-tuple-element.31), channel_id=1, source_target_pairs={{0,8},{8,16},{16,24},{24,32},{32,40},{40,48},{48,56},{56,64},{64,7... | collective-permute-start | bytes 663560 | tf_op jit(solution)/shard_map/ppermute | solution.py:446
  68.9 12.6 %collective-permute-start.3 = (f32[216,256]{1,0:T(8,128)}, f32[216,256]{1,0:T(8,128)S(1)}, u32[]{:S(2)}, u32[]{:S(2)}) collective-permute-start(f32[216,256]{1,0:T(8,128)} %get-tuple-element.32), channel_id=1, source_target_pairs={{8,0},{16,8},{24,16},{32,24},{40,32},{48,40},{56,48},{64,56},{72,6... | collective-permute-start | bytes 663560 | tf_op jit(solution)/shard_map/ppermute | solution.py:447
  74.2 7.3 %copy-start.1 = (f32[216,256]{1,0:T(8,128)}, f32[216,256]{1,0:T(8,128)S(1)}, u32[]{:S(2)}) copy-start(f32[216,256]{1,0:T(8,128)S(1)} %collective-permute-done.2.from_lower) | copy-start | bytes 663556
  81.5 0.7 copy-start.2
  81.5 0.8 copy-start
where the time goes:
time: 127 us; the launch traced here: 126 us
  Pallas kernels  67 us (53%)
  starting transfers between devices  29.7 us (23%)
  local copies, waits for them, and re-layouts  12.8 us (10%)
  waiting for transfers between devices  12 us (9%)
  between operations  2.51 us (2%)
  other arithmetic  2.14 us (2%)
    pallas_call x1, Pallas kernels, make_rate(): pl.pallas_call(rate_kernel, grid=(faces // TILE,), in_specs=[pl.BlockSpec...  42.7 us
    all_to_all x1, starting transfers between devices, body(): lax.all_to_all(least.reshape(devices), ('shock', 'trans'), split_axis=0,...  11.1 us
    ppermute x1, waiting for transfers between devices, body(): slab_upper = lax.ppermute(slab_down, 'shock', down)  7.33 us
    pallas_call x1, Pallas kernels, make_border(): pl.pallas_call(border_kernel, grid=(2,), in_specs=[pl.BlockSpec((1, 512),...  7.28 us
    pallas_call x1, Pallas kernels, make_fields(): pl.pallas_call(fields_kernel, grid=(elems // CHUNK,), in_specs=[pl.BlockS...  7.19 us
    unnamed x25, local copies, waits for them, and re-layouts  6.52 us
    pallas_call x1, Pallas kernels, make_weights(): pl.pallas_call(weights_kernel, out_shape=(jax.ShapeDtypeStruct((4 * ROWS,...  6.28 us
    ppermute x1, starting transfers between devices, body(): from_lower = lax.ppermute(to_upper, 'shock', up)  4.94 us
  transfers between devices with their start and end apart: 6, of which 3 were waited for; matrix products, arithmetic and copies ran while one was open for 10% of the time, Pallas kernels for 16%

commit v1 on v0

v1 whole, which is shorter than its diff:
```python
import functools

import jax
import jax.numpy as jnp
import numpy as np
from jax import lax
from jax.experimental import pallas as pl
from jax.experimental.pallas import tpu as pltpu
from jax.sharding import PartitionSpec as P

HIGHEST_PREC = lax.Precision.HIGHEST
CFL_NUMBER = 0.3
BF16 = jnp.bfloat16
F32 = jnp.float32

VARS = 11
BASIS = 10
FACE = 6
ROWS = 112
TROWS = 72
ELEM_BLOCK = 256
TILE = 512
CHUNK = 512


def expansion_tables():
    rows = np.arange(ROWS)
    outer = np.zeros((ROWS, 16), np.float32)
    inner = np.zeros((ROWS, 16), np.float32)
    live = rows < VARS * BASIS
    outer[rows[live], rows[live] // VARS] = 1.0
    inner[rows[live], rows[live] % VARS] = 1.0
    face_live = (np.arange(TROWS) < VARS * FACE).astype(np.float32)[:, None]
    outer_face = outer[:TROWS] * face_live
    inner_face = inner[:TROWS] * face_live
    thrice = lambda matrix: np.tile(matrix, (1, 3))
    bound = np.zeros((TROWS, ROWS), np.float32)
    bound[VARS * FACE, VARS * BASIS] = 1.0
    return (
        thrice(outer.T),
        thrice(inner.T),
        thrice(outer_face.T),
        thrice(inner_face.T),
        thrice(inner @ inner.T),
        thrice(inner_face @ inner.T),
        thrice(inner @ inner_face.T),
        thrice(outer_face @ outer_face.T),
        thrice(bound),
    )


def exact_dot(left, right, contract=((1,), (0,))):
    return lax.dot_general(
        left, right, (contract, ((), ())), precision=HIGHEST_PREC, preferred_element_type=F32
    )


def split3_cols(wide):
    third = wide.shape[1] // 3
    high = wide.astype(BF16).astype(F32)
    lane = lax.broadcasted_iota(jnp.int32, wide.shape, 1)
    return jnp.where(lane < 2 * third, high, wide - high).astype(BF16)


def weights_kernel(
    jac, der, res, lif, outer3, inner3, outer_face3, inner_face3, var_elem, var_trace, var_lift,
    basis_face, bound, w_elem, w_trace, w_flux, w_lift, small, wide_a, wide_b, face_a,
):
    small[...] = jnp.zeros_like(small)
    wide_a[...] = jnp.zeros_like(wide_a)
    wide_b[...] = jnp.zeros_like(wide_b)
    face_a[...] = jnp.zeros_like(face_a)
    for d in range(3):
        small[16 * d : 16 * d + VARS, 0:VARS] = jac[:, d, :]
        small[48 + 16 * d : 48 + 16 * d + BASIS, 0:BASIS] = der[:, d, :]
    for k in range(4):
        small[96 + 16 * k : 96 + 16 * k + FACE, 0:BASIS] = res[:, k, :]
        small[160 + 16 * k : 160 + 16 * k + FACE, 0:BASIS] = lif[:, k, :]
    jac_cols = exact_dot(small[0:48, :], inner3[...])
    jac_face_cols = exact_dot(small[0:48, :], inner_face3[...])
    other_cols = exact_dot(small[48:160, :], outer3[...])

    def repeat_rows(cols, first, target, count):
        for b in range(count):
            target[b * VARS : (b + 1) * VARS, :] = jnp.broadcast_to(
                cols[first + b : first + b + 1], (VARS, cols.shape[1])
            )

    def tile_rows(cols, first, target, count):
        for b in range(count):
            target[b * VARS : (b + 1) * VARS, :] = cols[first : first + VARS]

    total = None
    for d in range(3):
        repeat_rows(other_cols, 16 * d, wide_a, BASIS)
        tile_rows(jac_cols, 16 * d, wide_b, BASIS)
        term = wide_a[...] * wide_b[...]
        total = term if total is None else total + term
        w_elem[(d + 1) * ROWS : (d + 2) * ROWS, :] = split3_cols(wide_a[...] * var_elem[...])
        tile_rows(jac_face_cols, 16 * d, face_a, FACE)
        w_flux[d * TROWS : (d + 1) * TROWS, :] = split3_cols(face_a[0:TROWS] * basis_face[...])
    w_elem[0:ROWS, :] = split3_cols(total)
    for k in range(4):
        repeat_rows(other_cols, 48 + 16 * k, wide_a, FACE)
        w_trace[k * TROWS : (k + 1) * TROWS, :] = split3_cols(
            wide_a[0:TROWS] * var_trace[...] + bound[...]
        )
        lif_cols = exact_dot(
            small[160 + 16 * k : 176 + 16 * k, :], outer_face3[...], ((0,), (0,))
        )
        repeat_rows(lif_cols, 0, face_a, BASIS)
        w_lift[k * ROWS : (k + 1) * ROWS, :] = split3_cols(face_a[...] * var_lift[...])


def make_weights(jacobian, derivative, restriction, lifting):
    tables = [jnp.asarray(table) for table in expansion_tables()]
    return pl.pallas_call(
        weights_kernel,
        out_shape=(
            jax.ShapeDtypeStruct((4 * ROWS, 3 * ROWS), BF16),
            jax.ShapeDtypeStruct((4 * TROWS, 3 * ROWS), BF16),
            jax.ShapeDtypeStruct((3 * TROWS, 3 * TROWS), BF16),
            jax.ShapeDtypeStruct((4 * ROWS, 3 * TROWS), BF16),
        ),
        scratch_shapes=[
            pltpu.VMEM((224, 16), F32),
            pltpu.VMEM((ROWS, 3 * ROWS), F32),
            pltpu.VMEM((ROWS, 3 * ROWS), F32),
            pltpu.VMEM((ROWS, 3 * TROWS), F32),
        ],
        cost_estimate=pl.CostEstimate(flops=4_000_000, bytes_accessed=2_000_000, transcendentals=0),
        name="weights",
    )(
        jnp.transpose(jacobian, (1, 0, 2)),
        jnp.transpose(derivative, (1, 0, 2)),
        jnp.transpose(restriction, (1, 0, 2)),
        jnp.transpose(lifting, (2, 0, 1)),
        *tables,
    )


def lane_gather(table, tiles, index_row):
    wide = jnp.broadcast_to(index_row, (8, 128))
    low = wide & 127
    high = lax.shift_right_logical(wide, 7)
    picked = jnp.take_along_axis(table[:, 0:128], low, axis=1)
    for t in range(1, tiles):
        other = jnp.take_along_axis(table[:, t * 128 : (t + 1) * 128], low, axis=1)
        picked = jnp.where(high == t, other, picked)
    return picked


def share_kernel(velocity, share, to_lower, to_upper, table):
    table[...] = jnp.zeros_like(table)
    table[0:3, :] = velocity[...]
    tiles = velocity.shape[1] // 128
    to_lower[...] = lane_gather(table, tiles, share[0:1, :])
    to_upper[...] = lane_gather(table, tiles, share[1:2, :])


def mesh_kernel(velocity, from_lower, from_upper, corners, sizes, sounds, geom, least, table):
    own = velocity.shape[1]
    table[...] = jnp.zeros_like(table)
    table[0:3, 0:own] = velocity[...]
    table[:, own : own + 128] = from_lower[...]
    table[:, own + 128 : own + 256] = from_upper[...]
    tiles = (own + 256) // 128
    elems = corners.shape[1]
    for j in range(elems // 128):
        cols = slice(j * 128, (j + 1) * 128)
        total = None
        for corner in range(4):
            value = lane_gather(table, tiles, corners[corner : corner + 1, cols])
            total = value if total is None else total + value
        geom[:, cols] = total * 0.25
    moves = jnp.abs(geom[0:3, :])
    bound = sounds[...] + moves[0:1] + moves[1:2] + moves[2:3]
    geom[3:4, :] = bound
    geom[4:5, :] = 1.0 / sizes[...]
    least[...] = jnp.broadcast_to(
        jnp.min(sizes[...] / bound, axis=1, keepdims=True)[None], least.shape
    )


def split3_rows(value):
    high = value.astype(BF16)
    low = (value - high.astype(F32)).astype(BF16)
    return jnp.concatenate([high, low, high], axis=0)


def split2_rows(value):
    high = value.astype(BF16)
    low = (value - high.astype(F32)).astype(BF16)
    return jnp.concatenate([high, low], axis=0)


def apply_operator(pieces, geom, w_elem, cols):
    parts = jnp.dot(w_elem[...], pieces, preferred_element_type=F32)
    return (
        parts[0:ROWS]
        - geom[0:1, cols] * parts[ROWS : 2 * ROWS]
        - geom[1:2, cols] * parts[2 * ROWS : 3 * ROWS]
        - geom[2:3, cols] * parts[3 * ROWS : 4 * ROWS]
    ) * geom[4:5, cols]


def third_kernel(l2_ref, geom, w_elem, l3_out):
    l3_out[...] = apply_operator(split3_rows(l2_ref[...]), geom, w_elem, slice(None))


def make_third(second, geom, w_elem):
    elems = geom.shape[1]
    return pl.pallas_call(
        third_kernel,
        grid=(elems // CHUNK,),
        in_specs=[
            pl.BlockSpec((ROWS, CHUNK), lambda i: (0, i)),
            pl.BlockSpec((8, CHUNK), lambda i: (0, i)),
            pl.BlockSpec((4 * ROWS, 3 * ROWS), lambda i: (0, 0)),
        ],
        out_specs=pl.BlockSpec((ROWS, CHUNK), lambda i: (0, i)),
        out_shape=jax.ShapeDtypeStruct((ROWS, elems), F32),
        cost_estimate=pl.CostEstimate(
            flops=2 * 448 * 336 * elems, bytes_accessed=2_000_000, transcendentals=0
        ),
        name="third",
    )(second, geom, w_elem)


def build_selection(index_row, select):
    count = index_row.shape[1]
    low = index_row & (ELEM_BLOCK - 1)
    high = lax.shift_right_logical(index_row, 8)
    place = lax.broadcasted_iota(jnp.int32, (ELEM_BLOCK, count), 0)
    match = jnp.where(place == low, 1.0, 0.0).astype(BF16)
    for t in range(select.shape[0] // ELEM_BLOCK):
        here = jnp.where(high == t, 1.0, 0.0).astype(BF16)
        select[t * ELEM_BLOCK : (t + 1) * ELEM_BLOCK, :] = match * here


def choose(stacked, which, rows):
    value = stacked[0:rows]
    for k in range(1, 4):
        value = jnp.where(which == k, stacked[k * rows : (k + 1) * rows], value)
    return value


def traces_of(picked, which, w_trace):
    pieces = jnp.concatenate([picked, picked[0:ROWS]], axis=0)
    stacked = jnp.dot(w_trace[...], pieces, preferred_element_type=F32)
    return choose(stacked, which, TROWS)


def join_slab(ref):
    return jnp.concatenate([ref[0:1, :], ref[1:2, :]], axis=1)


def join_peers(value):
    wide = jnp.concatenate([value, value], axis=1)
    left = lax.broadcasted_iota(jnp.int32, (1, 128), 1) < 64
    return jnp.concatenate(
        [
            jnp.where(left, wide[2 * m : 2 * m + 1], wide[2 * m + 1 : 2 * m + 2])
            for m in range(4)
        ],
        axis=1,
    )


def front_kernel(
    state, geom, least, s_elem, s_face, p_elem, p_face, w_elem, w_trace, c_out, l1_out, l2_out,
    own, to_lower, to_upper, to_peer, table, select,
):
    step = pl.program_id(0)
    chunks = table.shape[1] // CHUNK

    @pl.when(step < chunks)
    def _():
        cols = pl.ds(pl.multiple_of(step * CHUNK, CHUNK), CHUNK)
        for b in range(BASIS):
            c_out[b * VARS : (b + 1) * VARS, :] = state[b]
        c_out[BASIS * VARS : BASIS * VARS + 1, :] = geom[3:4, cols]
        c_out[BASIS * VARS + 1 : ROWS, :] = jnp.zeros((1, CHUNK), F32)
        pieces = split3_rows(c_out[...])
        table[0 : 2 * ROWS, cols] = pieces[0 : 2 * ROWS]
        l1_out[...] = apply_operator(pieces, geom, w_elem, cols)
        pieces = split3_rows(l1_out[...])
        table[2 * ROWS : 4 * ROWS, cols] = pieces[0 : 2 * ROWS]
        l2_out[...] = apply_operator(pieces, geom, w_elem, cols)
        table[4 * ROWS : 6 * ROWS, cols] = split2_rows(l2_out[...])

    def border(index_row, which):
        build_selection(index_row, select)
        picked = jnp.dot(table[...], select[...], preferred_element_type=F32).astype(BF16)
        own[3 * TROWS :, :] = jnp.zeros((8, own.shape[1]), F32)
        for i in range(3):
            own[i * TROWS : (i + 1) * TROWS, :] = traces_of(
                picked[2 * ROWS * i : 2 * ROWS * (i + 1)], which, w_trace
            )

    @pl.when(step == chunks)
    def _():
        border(join_slab(s_elem), join_slab(s_face))
        to_lower[...] = own[0 : 3 * TROWS, 0:256]
        to_upper[...] = own[0 : 3 * TROWS, 256:512]

    @pl.when(step == chunks + 1)
    def _():
        border(join_peers(p_elem[...]), join_peers(p_face[...]))
        lane = lax.broadcasted_iota(jnp.int32, (ROWS, 128), 1)
        left = lane < 64
        spare = (lax.broadcasted_iota(jnp.int32, (ROWS, 128), 0) == ROWS - 1) & (lane >= 64)
        smallest = jnp.min(least[...])
        for m in range(4):
            top = own[0:ROWS, m * 128 : (m + 1) * 128]
            bottom = own[ROWS : 2 * ROWS, m * 128 : (m + 1) * 128]
            one = jnp.where(left, top, pltpu.roll(bottom, 64, 1))
            two = jnp.where(left, pltpu.roll(top, 64, 1), bottom)
            to_peer[2 * m] = jnp.where(spare, smallest, one)
            to_peer[2 * m + 1] = jnp.where(spare, smallest, two)


def make_front(state, geom, least, border_index, w_elem, w_trace):
    elems = geom.shape[1]
    chunks = elems // CHUNK
    full = jax.ShapeDtypeStruct((ROWS, elems), F32)
    block = pl.BlockSpec((ROWS, CHUNK), lambda i: (0, jnp.minimum(i, chunks - 1)))
    whole = pl.BlockSpec(memory_space=pltpu.VMEM)
    return pl.pallas_call(
        front_kernel,
        grid=(chunks + 2,),
        in_specs=[pl.BlockSpec((BASIS, VARS, CHUNK), lambda i: (0, 0, jnp.minimum(i, chunks - 1)))]
        + [whole] * 8,
        out_specs=[
            block,
            block,
            block,
            pl.BlockSpec((2 * ROWS, 512), lambda i: (0, jnp.maximum(i - chunks, 0))),
            whole,
            whole,
            whole,
        ],
        out_shape=[full] * 3
        + [
            jax.ShapeDtypeStruct((2 * ROWS, 1024), F32),
            jax.ShapeDtypeStruct((3 * TROWS, 256), F32),
            jax.ShapeDtypeStruct((3 * TROWS, 256), F32),
            jax.ShapeDtypeStruct((8, ROWS, 128), F32),
        ],
        scratch_shapes=[pltpu.VMEM((6 * ROWS, elems), BF16), pltpu.VMEM((elems, 512), BF16)],
        name="front",
    )(state, geom, least, *border_index, w_elem, w_trace)


def flux_parts(own, theirs, normal, w_flux):
    jump = theirs - own
    bound = jnp.maximum(own[66:67], theirs[66:67])
    parts = jnp.dot(w_flux[...], split3_rows(jump), preferred_element_type=F32)
    central = (
        normal[0:1] * parts[0:TROWS]
        + normal[1:2] * parts[TROWS : 2 * TROWS]
        + normal[2:3] * parts[2 * TROWS : 3 * TROWS]
    )
    return central, bound * jump


def lift_values(values, which, w_lift):
    stacked = jnp.dot(w_lift[...], split3_rows(values), preferred_element_type=F32)
    return split2_rows(choose(stacked, which, ROWS))


def add_selected(pieces, select, total):
    total[...] += lax.dot_general(
        pieces, select[...], (((1,), (1,)), ((), ())), preferred_element_type=F32
    )


def combine(first, second, third, half, sixth):
    return first + half * second + sixth * third


def rate_kernel(
    c_ref, l1_ref, l2_ref, l3_ref, geom, own, from_lower, from_upper, from_peer, s_elem, s_face,
    s_normal, p_elem, p_face, p_normal, p_count, elem, face, normal, w_trace, w_flux, w_lift, out,
    step_out, table, total, even, odd, theirs, lifted,
):
    step = pl.program_id(0)
    last_tile = elem.shape[1] // TILE - 1
    tau = CFL_NUMBER * jnp.min(from_peer[:, ROWS - 1 : ROWS, 64:128])
    half = -0.5 * tau
    sixth = tau * tau / 6.0

    def sides(tile):
        cols = pl.ds(pl.multiple_of(tile * TILE, TILE), TILE)
        index_row = jnp.concatenate([elem[0:1, cols], elem[1:2, cols]], axis=1)
        which = jnp.concatenate([face[0:1, cols], face[1:2, cols]], axis=1)
        return index_row, which

    def inner_values(tile, traces):
        cols = pl.ds(pl.multiple_of(tile * TILE, TILE), TILE)
        central, upwind = flux_parts(traces[:, 0:TILE], traces[:, TILE:], normal[:, cols], w_flux)
        return jnp.concatenate([0.5 * (central - upwind), 0.5 * (central + upwind)], axis=1)

    @pl.when(step == 0)
    def _():
        step_out[0, 0] = tau
        total[...] = jnp.zeros_like(total)
        for j in range(c_ref.shape[1] // CHUNK):
            cols = slice(j * CHUNK, (j + 1) * CHUNK)
            table[:, cols] = split2_rows(
                combine(c_ref[:, cols], l1_ref[:, cols], l2_ref[:, cols], half, sixth)
            )
        left = lax.broadcasted_iota(jnp.int32, (ROWS, 128), 1) < 64
        theirs[0 : 3 * TROWS, 0:256] = from_lower[...]
        theirs[0 : 3 * TROWS, 256:512] = from_upper[...]
        for m in range(4):
            cols = slice(512 + m * 128, 512 + (m + 1) * 128)
            one, two = from_peer[2 * m], from_peer[2 * m + 1]
            theirs[0:ROWS, cols] = jnp.where(left, one, pltpu.roll(two, 64, 1))
            theirs[ROWS : 2 * ROWS, cols] = jnp.where(left, pltpu.roll(one, 64, 1), two)
        slots = lax.broadcasted_iota(jnp.int32, p_elem.shape, 1)
        alive = jnp.where(slots < p_count[...], 1.0, 0.0)
        b_elem = jnp.concatenate([join_slab(s_elem), join_peers(p_elem[...])], axis=1)
        b_face = jnp.concatenate([join_slab(s_face), join_peers(p_face[...])], axis=1)
        b_live = jnp.concatenate([jnp.ones((1, 512), F32), join_peers(alive)], axis=1)
        b_normal = jnp.concatenate(
            [
                jnp.concatenate([join_slab(s_normal.at[d]), join_peers(p_normal[d])], axis=1)
                for d in range(3)
            ],
            axis=0,
        )
        build_selection(b_elem, odd)
        index_row, _ = sides(0)
        build_selection(index_row, even)

        def merged(ref):
            return combine(
                ref[0:TROWS], ref[TROWS : 2 * TROWS], ref[2 * TROWS : 3 * TROWS], half, sixth
            )

        central, upwind = flux_parts(merged(own), merged(theirs), b_normal, w_flux)
        values = (0.5 * (central - upwind)) * b_live
        lifted[...] = lift_values(values, b_face, w_lift)
        add_selected(lifted[...], odd, total)
    for parity in range(2):
        tile = 2 * step + parity
        cur, nxt = (even, odd) if parity == 0 else (odd, even)
        picked = jnp.dot(table[...], cur[...], preferred_element_type=F32).astype(BF16)
        index_next, _ = sides(jnp.minimum(tile + 1, last_tile))
        build_selection(index_next, nxt)
        _, which = sides(tile)
        values = inner_values(tile, traces_of(picked, which, w_trace))
        add_selected(lift_values(values, which, w_lift), cur, total)
    @pl.when(step == pl.num_programs(0) - 1)
    def _():
        for j in range(c_ref.shape[1] // CHUNK):
            cols = slice(j * CHUNK, (j + 1) * CHUNK)
            summed = total[0:ROWS, cols] + total[ROWS : 2 * ROWS, cols]
            volume = combine(l1_ref[:, cols], l2_ref[:, cols], l3_ref[:, cols], half, sixth)
            rate = -(volume + summed * geom[4:5, cols])
            for b in range(BASIS):
                out[b, :, cols] = rate[b * VARS : (b + 1) * VARS]


def make_rate(fields, geom, own, received, border, inner, weights):
    elems = geom.shape[1]
    faces = inner[0].shape[1]
    whole = pl.BlockSpec(memory_space=pltpu.VMEM)
    return pl.pallas_call(
        rate_kernel,
        grid=(faces // TILE // 2,),
        in_specs=[whole] * 22,
        out_specs=(whole, pl.BlockSpec(memory_space=pltpu.SMEM)),
        out_shape=(
            jax.ShapeDtypeStruct((BASIS, VARS, elems), F32),
            jax.ShapeDtypeStruct((1, 1), F32),
        ),
        scratch_shapes=[
            pltpu.VMEM((2 * ROWS, elems), BF16),
            pltpu.VMEM((2 * ROWS, elems), F32),
            pltpu.VMEM((elems, 2 * TILE), BF16),
            pltpu.VMEM((elems, 2 * TILE), BF16),
            pltpu.VMEM((2 * ROWS, 1024), F32),
            pltpu.VMEM((2 * ROWS, 2 * TILE), BF16),
        ],
        name="rate",
    )(*fields, geom, own, *received, *border, *inner, *weights)


def body(
    conserved,
    cell_size,
    sound_speed,
    jacobian,
    derivative,
    restriction,
    lifting,
    vertex_velocity,
    share_index,
    elem_vertex,
    inner_elem,
    inner_face,
    inner_normal,
    slab_elem,
    slab_face,
    slab_normal,
    peer_elem,
    peer_face,
    peer_normal,
    peer_count,
):
    elems = conserved.shape[2]
    slabs = lax.axis_size("shock")
    up = [(i, i + 1) for i in range(slabs - 1)]
    down = [(i + 1, i) for i in range(slabs - 1)]

    shared = jax.ShapeDtypeStruct((8, 128), F32)
    to_lower, to_upper = pl.pallas_call(
        share_kernel,
        out_shape=(shared, shared),
        scratch_shapes=[pltpu.VMEM((8, vertex_velocity.shape[1]), F32)],
        name="share",
    )(vertex_velocity, share_index)
    from_lower = lax.ppermute(to_upper, "shock", up)
    from_upper = lax.ppermute(to_lower, "shock", down)
    w_elem, w_trace, w_flux, w_lift = make_weights(jacobian, derivative, restriction, lifting)
    geom, least = pl.pallas_call(
        mesh_kernel,
        out_shape=(
            jax.ShapeDtypeStruct((8, elems), F32),
            jax.ShapeDtypeStruct((slabs, 1, 128), F32),
        ),
        scratch_shapes=[pltpu.VMEM((8, vertex_velocity.shape[1] + 256), F32)],
        name="mesh",
    )(
        vertex_velocity,
        from_lower,
        from_upper,
        elem_vertex,
        cell_size.reshape(1, elems),
        sound_speed.reshape(1, elems),
    )
    slab_least = lax.all_to_all(least, "shock", split_axis=0, concat_axis=0, tiled=True)

    state = jnp.transpose(conserved, (1, 0, 2))
    first, second, third, own, slab_down, slab_up, peer_send = make_front(
        state, geom, slab_least, (slab_elem, slab_face, peer_elem, peer_face), w_elem, w_trace
    )
    slab_lower = lax.ppermute(slab_up, "shock", up)
    slab_upper = lax.ppermute(slab_down, "shock", down)
    peer_recv = lax.all_to_all(peer_send, "trans", split_axis=0, concat_axis=0, tiled=True)
    fourth = make_third(third, geom, w_elem)
    rate, step_size = make_rate(
        (first, second, third, fourth),
        geom,
        own,
        (slab_lower, slab_upper, peer_recv),
        (slab_elem, slab_face, slab_normal, peer_elem, peer_face, peer_normal, peer_count),
        (inner_elem, inner_face, inner_normal),
        (w_trace, w_flux, w_lift),
    )
    return (jnp.transpose(rate, (1, 0, 2)), step_size.reshape(()))


def solution(mesh):
    return jax.shard_map(
        body,
        mesh=mesh,
        in_specs=(
            P(None, None, ("shock", "trans")),
            P(("shock", "trans")),
            P(("shock", "trans")),
            P(),
            P(),
            P(),
            P(),
            P(None, ("shock", "trans")),
            P(None, ("shock", "trans")),
            P(None, ("shock", "trans")),
            P(None, ("shock", "trans")),
            P(None, ("shock", "trans")),
            P(None, ("shock", "trans")),
            P(None, ("shock", "trans")),
            P(None, ("shock", "trans")),
            P(None, None, ("shock", "trans")),
            P(None, ("shock", "trans")),
            P(None, ("shock", "trans")),
            P(None, None, ("shock", "trans")),
            P(None, ("shock", "trans")),
        ),
        out_specs=(P(None, None, ("shock", "trans")), P()),
        check_vma=False,
    )
```

time: 127 us -> 104 us (0.82)
  the two profiles are of different devices: /device:TPU:110 before, /device:TPU:14 now
where the time goes in v1:
time: 104 us; the launch traced here: 103 us
  Pallas kernels  56.6 us (54%)
  starting transfers between devices  28 us (27%)
  waiting for transfers between devices  14.9 us (14%)
  local copies, waits for them, and re-layouts  2.71 us (3%)
    pallas_call x1, Pallas kernels, make_rate(): pl.pallas_call(rate_kernel, grid=(faces // TILE // 2,), in_specs=[whole]...  34.7 us
    all_to_all x1, starting transfers between devices, body(): lax.all_to_all(least, 'shock', split_axis=0, concat_axis=0, tiled=True)  11.2 us
    pallas_call x1, Pallas kernels, make_front(): pl.pallas_call(front_kernel, grid=(chunks + 2,), in_specs=[pl.BlockSpec((...  11.1 us
    ppermute x1, waiting for transfers between devices, body(): from_upper = lax.ppermute(to_lower, 'shock', down)  5.69 us
    all_to_all x1, waiting for transfers between devices, body(): lax.all_to_all(least, 'shock', split_axis=0, concat_axis=0, tiled=True)  4.99 us
    all_to_all x1, starting transfers between devices, body(): lax.all_to_all(peer_send, 'trans', split_axis=0, concat_axis=0, tiled=True)  4.92 us
    pallas_call x1, Pallas kernels, make_third(): pl.pallas_call(third_kernel, grid=(elems // CHUNK,), in_specs=[pl.BlockSp...  4.33 us
    ppermute x1, waiting for transfers between devices, body(): slab_upper = lax.ppermute(slab_down, 'shock', down)  4.25 us
  transfers between devices with their start and end apart: 6, of which 3 were waited for; matrix products, arithmetic and copies ran while one was open for 1% of the time, Pallas kernels for 7%

profile of v1, /device:TPU:14, one launch (start us, length us, event | category | flops | bytes accessed | tf_op | source)
XLA Modules:
  0.0 103.1 jit_solution(2919311267814122892)
XLA Ops:
  0.6 1.4 %share.2 = (f32[8,128]{1,0:T(8,128)}, f32[8,128]{1,0:T(8,128)}) custom-call(f32[3,512]{1,0:T(4,128)} %velocity.3, s32[2,128]{1,0:T(2,128)} %share.3), custom_call_target="tpu_custom_call" | custom-call | tf_op jit(solution)/shard_map/share/pallas_call | solution.py:519
  2.0 3.7 %collective-permute-start = (f32[8,128]{1,0:T(8,128)}, f32[8,128]{1,0:T(8,128)S(1)}, u32[]{:S(2)}, u32[]{:S(2)}) collective-permute-start(f32[8,128]{1,0:T(8,128)} %get-tuple-element.19), channel_id=1, source_target_pairs={{0,8},{8,16},{16,24},{24,32},{32,40},{40,48},{48,56},{56,64},{64,7... | collective-permute-start | bytes 12296 | tf_op jit(solution)/shard_map/ppermute | solution.py:525
  5.7 2.1 %collective-permute-start.1 = (f32[8,128]{1,0:T(8,128)}, f32[8,128]{1,0:T(8,128)S(1)}, u32[]{:S(2)}, u32[]{:S(2)}) collective-permute-start(f32[8,128]{1,0:T(8,128)} %get-tuple-element.20), channel_id=1, source_target_pairs={{8,0},{16,8},{24,16},{32,24},{40,32},{48,40},{56,48},{64,56},{72,6... | collective-permute-start | bytes 12296 | tf_op jit(solution)/shard_map/ppermute | solution.py:526
  7.9 0.0 collective-permute-done.from_lower
  7.9 0.0 copy-start.4
  7.9 5.7 %collective-permute-done.1.from_upper = f32[8,128]{1,0:T(8,128)S(1)} collective-permute-done((f32[8,128]{1,0:T(8,128)}, f32[8,128]{1,0:T(8,128)S(1)}, u32[]{:S(2)}, u32[]{:S(2)}) %collective-permute-start.1) | collective-permute-done | bytes 4128 | tf_op jit(solution)/shard_map/ppermute | solution.py:526
  13.6 0.0 copy-start.5
  13.6 0.0 copy-done.4
  13.6 0.6 copy-done.5
  14.2 2.2 %mesh.1 = (f32[8,2048]{1,0:T(8,128)}, f32[32,1,128]{2,1,0:T(1,128)}) custom-call(f32[3,512]{1,0:T(4,128)} %velocity.3, f32[8,128]{1,0:T(8,128)} %copy-done.4, f32[8,128]{1,0:T(8,128)} %copy-done.5, s32[4,2048]{1,0:T(4,128)} %corners.1, f32[1,2048]{1,0:T(1,128)} %bitcast.14, f32[1,2048]{1,0:T(1,128)} %bitcast.15), custom_call_target="tpu_custom_call" | custom-call | tf_op jit(solution)/shard_map/mesh/pallas_call | solution.py:528
  16.4 11.2 %all-to-all-start = ((f32[32,1,128]{2,1,0:T(1,128)}), f32[32,1,128]{2,1,0:T(1,128)S(1)}, u32[]{:S(2)}, u32[]{:S(2)}) async-start(f32[32,1,128]{2,1,0:T(1,128)} %get-tuple-element.22), calls=%async_computation | async-start | bytes 32768 | tf_op jit(solution)/shard_map/all_to_all | solution.py:544
  27.5 2.9 %weights.1 = (bf16[448,336]{1,0:T(8,128)(2,1)}, bf16[288,336]{1,0:T(8,128)(2,1)}, bf16[216,216]{1,0:T(8,128)(2,1)}, bf16[448,216]{1,0:T(8,128)(2,1)}) custom-call(f32[11,3,11]{2,1,0:T(4,128)} %bitcast.10, f32[10,3,10]{2,1,0:T(4,128)} %bitcast.11, f32[6,4,10]{2,1,0:T(4,128)} %bitcast.12, f32[6,4,10]{2,1,0:T(4,128)} %bitcast.13, ...), custom_call_target="tpu_custom_call" | custom-call | flops 4000000 | bytes 2000000 | tf_op jit(solution)/shard_map/weights/pallas_call | solution.py:117
  30.5 5.0 %all-to-all-done.least = f32[32,1,128]{2,1,0:T(1,128)S(1)} async-done(((f32[32,1,128]{2,1,0:T(1,128)}), f32[32,1,128]{2,1,0:T(1,128)S(1)}, u32[]{:S(2)}, u32[]{:S(2)}) %all-to-all-start) | async-done | bytes 16416 | tf_op jit(solution)/shard_map/all_to_all | solution.py:544
  35.4 0.0 copy-start.3
  35.4 0.6 copy-done.3
  36.0 0.0 copy-start.6
  36.0 11.1 %front.1 = (f32[112,2048]{1,0:T(8,128)}, f32[112,2048]{1,0:T(8,128)}, f32[112,2048]{1,0:T(8,128)}, f32[224,1024]{1,0:T(8,128)}, f32[216,256]{1,0:T(8,128)}, /*index=5*/f32[216,256]{1,0:T(8,128)}, f32[8,112,128]{2,1,0:T(8,128)}) custom-call(f32[10,11,2048]{2,1,0:T(8,128)} %bitcast.9, f32[8,2048]{1,0:T(8,128)} %get-tuple-element.21.geom, ...), custom_call_target="tpu_custom_call" | custom-call | tf_op jit(solution)/shard_map/front/pallas_call | solution.py:329
  47.1 4.9 %all-to-all-start.1 = ((f32[8,112,128]{2,1,0:T(8,128)}), f32[8,112,128]{2,1,0:T(8,128)S(1)}, u32[]{:S(2)}, u32[]{:S(2)}) async-start(f32[8,112,128]{2,1,0:T(8,128)} %get-tuple-element.31), calls=%async_computation.1 | async-start | bytes 917504 | tf_op jit(solution)/shard_map/all_to_all | solution.py:552
  52.1 4.0 %collective-permute-start.2 = (f32[216,256]{1,0:T(8,128)}, f32[216,256]{1,0:T(8,128)S(1)}, u32[]{:S(2)}, u32[]{:S(2)}) collective-permute-start(f32[216,256]{1,0:T(8,128)} %get-tuple-element.29), channel_id=1, source_target_pairs={{0,8},{8,16},{16,24},{24,32},{32,40},{40,48},{48,56},{56,64},{64,7... | collective-permute-start | bytes 663560 | tf_op jit(solution)/shard_map/ppermute | solution.py:550
  56.0 2.1 %collective-permute-start.3 = (f32[216,256]{1,0:T(8,128)}, f32[216,256]{1,0:T(8,128)S(1)}, u32[]{:S(2)}, u32[]{:S(2)}) collective-permute-start(f32[216,256]{1,0:T(8,128)} %get-tuple-element.30), channel_id=1, source_target_pairs={{8,0},{16,8},{24,16},{32,24},{40,32},{48,40},{56,48},{64,56},{72,6... | collective-permute-start | bytes 663560 | tf_op jit(solution)/shard_map/ppermute | solution.py:551
  58.1 0.0 copy-done.6
  58.1 0.7 copy.31.p_count
  58.8 4.3 %third.1.l3_ref = f32[112,2048]{1,0:T(8,128)} custom-call(f32[112,2048]{1,0:T(8,128)} %get-tuple-element.27.l2_ref, f32[8,2048]{1,0:T(8,128)} %get-tuple-element.21.geom, bf16[448,336]{1,0:T(8,128)(2,1)} %get-tuple-element.23.w_elem), custom_call_target="tpu_custom_call" | custom-call | flops 616562688 | bytes 2000000 | tf_op jit(solution)/shard_map/third/pallas_call | solution.py:213
  63.2 0.0 collective-permute-done.2.from_lower
  63.2 0.0 copy-start.1
  63.2 4.3 %collective-permute-done.3.from_upper = f32[216,256]{1,0:T(8,128)S(1)} collective-permute-done((f32[216,256]{1,0:T(8,128)}, f32[216,256]{1,0:T(8,128)S(1)}, u32[]{:S(2)}, u32[]{:S(2)}) %collective-permute-start.3) | collective-permute-done | bytes 221216 | tf_op jit(solution)/shard_map/ppermute | solution.py:551
  67.4 0.0 copy-start.2
  67.4 0.0 all-to-all-done.1.from_peer
  67.4 0.0 copy-start
  67.4 0.0 copy-done.1
  67.4 0.7 copy-done.2
  68.1 0.2 copy-done
  68.3 34.7 %rate.1 = (f32[10,11,2048]{2,1,0:T(8,128)}, f32[1,1]{1,0:T(1,128)}) custom-call(f32[112,2048]{1,0:T(8,128)} %get-tuple-element.25.c_ref, f32[112,2048]{1,0:T(8,128)} %get-tuple-element.26.l1_ref, f32[112,2048]{1,0:T(8,128)} %get-tuple-element.27.l2_ref, f32[112,2048]{1,0:T(8,128)} %third.1.l3_ref, f32[8,2048]{1,0:T(8,128)} %get-tuple-element.21.geom, ...), custom_call_target="tpu_custom_call" | custom-call | tf_op jit(solution)/shard_map/rate/pallas_call | solution.py:470
Async XLA Ops:
  2.0 5.8 %collective-permute-start = (f32[8,128]{1,0:T(8,128)}, f32[8,128]{1,0:T(8,128)S(1)}, u32[]{:S(2)}, u32[]{:S(2)}) collective-permute-start(f32[8,128]{1,0:T(8,128)} %get-tuple-element.19), channel_id=1, source_target_pairs={{0,8},{8,16},{16,24},{24,32},{32,40},{40,48},{48,56},{56,64},{64,7... | collective-permute-start | bytes 12296 | tf_op jit(solution)/shard_map/ppermute | solution.py:525
  5.7 7.8 %collective-permute-start.1 = (f32[8,128]{1,0:T(8,128)}, f32[8,128]{1,0:T(8,128)S(1)}, u32[]{:S(2)}, u32[]{:S(2)}) collective-permute-start(f32[8,128]{1,0:T(8,128)} %get-tuple-element.20), channel_id=1, source_target_pairs={{8,0},{16,8},{24,16},{32,24},{40,32},{48,40},{56,48},{64,56},{72,6... | collective-permute-start | bytes 12296 | tf_op jit(solution)/shard_map/ppermute | solution.py:526
  7.9 5.7 %copy-start.4 = (f32[8,128]{1,0:T(8,128)}, f32[8,128]{1,0:T(8,128)S(1)}, u32[]{:S(2)}) copy-start(f32[8,128]{1,0:T(8,128)S(1)} %collective-permute-done.from_lower) | copy-start | bytes 12292
  13.6 0.6 copy-start.5
  16.4 19.1 %all-to-all-start = ((f32[32,1,128]{2,1,0:T(1,128)}), f32[32,1,128]{2,1,0:T(1,128)S(1)}, u32[]{:S(2)}, u32[]{:S(2)}) async-start(f32[32,1,128]{2,1,0:T(1,128)} %get-tuple-element.22), calls=%async_computation | async-start | bytes 32768 | tf_op jit(solution)/shard_map/all_to_all | solution.py:544
  35.4 0.6 copy-start.3
  36.0 22.1 %copy-start.6 = (s32[8,1]{0,1:T(1,128)S(1)}, s32[8,1]{0,1:T(1,128)}, u32[]{:S(2)}) copy-start(s32[8,1]{0,1:T(1,128)} %param.48) | copy-start | bytes 100
  47.1 20.3 %all-to-all-start.1 = ((f32[8,112,128]{2,1,0:T(8,128)}), f32[8,112,128]{2,1,0:T(8,128)S(1)}, u32[]{:S(2)}, u32[]{:S(2)}) async-start(f32[8,112,128]{2,1,0:T(8,128)} %get-tuple-element.31), calls=%async_computation.1 | async-start | bytes 917504 | tf_op jit(solution)/shard_map/all_to_all | solution.py:552
  52.1 11.1 %collective-permute-start.2 = (f32[216,256]{1,0:T(8,128)}, f32[216,256]{1,0:T(8,128)S(1)}, u32[]{:S(2)}, u32[]{:S(2)}) collective-permute-start(f32[216,256]{1,0:T(8,128)} %get-tuple-element.29), channel_id=1, source_target_pairs={{0,8},{8,16},{16,24},{24,32},{32,40},{40,48},{48,56},{56,64},{64,7... | collective-permute-start | bytes 663560 | tf_op jit(solution)/shard_map/ppermute | solution.py:550
  56.0 11.4 %collective-permute-start.3 = (f32[216,256]{1,0:T(8,128)}, f32[216,256]{1,0:T(8,128)S(1)}, u32[]{:S(2)}, u32[]{:S(2)}) collective-permute-start(f32[216,256]{1,0:T(8,128)} %get-tuple-element.30), channel_id=1, source_target_pairs={{8,0},{16,8},{24,16},{32,24},{40,32},{48,40},{56,48},{64,56},{72,6... | collective-permute-start | bytes 663560 | tf_op jit(solution)/shard_map/ppermute | solution.py:551
  63.2 4.3 %copy-start.1 = (f32[216,256]{1,0:T(8,128)}, f32[216,256]{1,0:T(8,128)S(1)}, u32[]{:S(2)}) copy-start(f32[216,256]{1,0:T(8,128)S(1)} %collective-permute-done.2.from_lower) | copy-start | bytes 663556
  67.4 0.7 copy-start.2
  67.4 0.8 copy-start

commit v2 on v1

--- a/solution.py
+++ b/solution.py
@@ -19,7 +19,7 @@
 ROWS = 112
 TROWS = 72
 ELEM_BLOCK = 256
-TILE = 512
+TILE = 1024
 CHUNK = 512
 
 
@@ -158,7 +158,10 @@
     to_upper[...] = lane_gather(table, tiles, share[1:2, :])
 
 
-def mesh_kernel(velocity, from_lower, from_upper, corners, sizes, sounds, geom, least, table):
+def mesh_kernel(
+    velocity, from_lower, from_upper, corners, sizes, sounds, after, geom, least, table
+):
+    del after
     own = velocity.shape[1]
     table[...] = jnp.zeros_like(table)
     table[0:3, 0:own] = velocity[...]
@@ -268,8 +271,8 @@
 
 
 def front_kernel(
-    state, geom, least, s_elem, s_face, p_elem, p_face, w_elem, w_trace, c_out, l1_out, l2_out,
-    own, to_lower, to_upper, to_peer, table, select,
+    state, geom, s_elem, s_face, p_elem, p_face, w_elem, w_trace, c_out, l1_out, l2_out, own,
+    to_lower, to_upper, to_peer, table, select,
 ):
     step = pl.program_id(0)
     chunks = table.shape[1] // CHUNK
@@ -288,10 +291,15 @@
         table[2 * ROWS : 4 * ROWS, cols] = pieces[0 : 2 * ROWS]
         l2_out[...] = apply_operator(pieces, geom, w_elem, cols)
         table[4 * ROWS : 6 * ROWS, cols] = split2_rows(l2_out[...])
-
-    def border(index_row, which):
-        build_selection(index_row, select)
-        picked = jnp.dot(table[...], select[...], preferred_element_type=F32).astype(BF16)
+        index_row = jnp.where(step == 0, join_slab(s_elem), join_peers(p_elem[...]))
+        half = select.at[:, pl.ds(pl.multiple_of(jnp.minimum(step, 1) * 512, 512), 512)]
+
+        @pl.when(step < 2)
+        def _():
+            build_selection(index_row, half)
+
+    def border(half, which):
+        picked = jnp.dot(table[...], half[...], preferred_element_type=F32).astype(BF16)
         own[3 * TROWS :, :] = jnp.zeros((8, own.shape[1]), F32)
         for i in range(3):
             own[i * TROWS : (i + 1) * TROWS, :] = traces_of(
@@ -300,27 +308,22 @@
 
     @pl.when(step == chunks)
     def _():
-        border(join_slab(s_elem), join_slab(s_face))
+        border(select.at[:, 0:512], join_slab(s_face))
         to_lower[...] = own[0 : 3 * TROWS, 0:256]
         to_upper[...] = own[0 : 3 * TROWS, 256:512]
 
     @pl.when(step == chunks + 1)
     def _():
-        border(join_peers(p_elem[...]), join_peers(p_face[...]))
-        lane = lax.broadcasted_iota(jnp.int32, (ROWS, 128), 1)
-        left = lane < 64
-        spare = (lax.broadcasted_iota(jnp.int32, (ROWS, 128), 0) == ROWS - 1) & (lane >= 64)
-        smallest = jnp.min(least[...])
+        border(select.at[:, 512:1024], join_peers(p_face[...]))
+        left = lax.broadcasted_iota(jnp.int32, (ROWS, 128), 1) < 64
         for m in range(4):
             top = own[0:ROWS, m * 128 : (m + 1) * 128]
             bottom = own[ROWS : 2 * ROWS, m * 128 : (m + 1) * 128]
-            one = jnp.where(left, top, pltpu.roll(bottom, 64, 1))
-            two = jnp.where(left, pltpu.roll(top, 64, 1), bottom)
-            to_peer[2 * m] = jnp.where(spare, smallest, one)
-            to_peer[2 * m + 1] = jnp.where(spare, smallest, two)
-
-
-def make_front(state, geom, least, border_index, w_elem, w_trace):
+            to_peer[2 * m] = jnp.where(left, top, pltpu.roll(bottom, 64, 1))
+            to_peer[2 * m + 1] = jnp.where(left, pltpu.roll(top, 64, 1), bottom)
+
+
+def make_front(state, geom, border_index, w_elem, w_trace):
     elems = geom.shape[1]
     chunks = elems // CHUNK
     full = jax.ShapeDtypeStruct((ROWS, elems), F32)
@@ -330,7 +333,7 @@
         front_kernel,
         grid=(chunks + 2,),
         in_specs=[pl.BlockSpec((BASIS, VARS, CHUNK), lambda i: (0, 0, jnp.minimum(i, chunks - 1)))]
-        + [whole] * 8,
+        + [whole] * 7,
         out_specs=[
             block,
             block,
@@ -347,9 +350,28 @@
             jax.ShapeDtypeStruct((3 * TROWS, 256), F32),
             jax.ShapeDtypeStruct((8, ROWS, 128), F32),
         ],
-        scratch_shapes=[pltpu.VMEM((6 * ROWS, elems), BF16), pltpu.VMEM((elems, 512), BF16)],
+        scratch_shapes=[pltpu.VMEM((6 * ROWS, elems), BF16), pltpu.VMEM((elems, 1024), BF16)],
         name="front",
-    )(state, geom, least, *border_index, w_elem, w_trace)
+    )(state, geom, *border_index, w_elem, w_trace)
+
+
+def stamp_kernel(least, value, out):
+    row = lax.broadcasted_iota(jnp.int32, value.shape, 1)
+    lane = lax.broadcasted_iota(jnp.int32, value.shape, 2)
+    out[...] = jnp.where((row == 7) & (lane >= 64), jnp.min(least[...]), value[...])
+
+
+def make_stamp(least, to_peer):
+    block = pl.BlockSpec((8, 8, 128), lambda i: (0, ROWS // 8 - 1, 0))
+    return pl.pallas_call(
+        stamp_kernel,
+        grid=(1,),
+        in_specs=[pl.BlockSpec(memory_space=pltpu.VMEM), block],
+        out_specs=block,
+        out_shape=jax.ShapeDtypeStruct(to_peer.shape, F32),
+        input_output_aliases={1: 0},
+        name="stamp",
+    )(least, to_peer)
 
 
 def flux_parts(own, theirs, normal, w_flux):
@@ -380,9 +402,9 @@
 
 
 def rate_kernel(
-    c_ref, l1_ref, l2_ref, l3_ref, geom, own, from_lower, from_upper, from_peer, s_elem, s_face,
+    c_any, l1_any, l2_any, l3_any, geom, own, from_lower, from_upper, from_peer, s_elem, s_face,
     s_normal, p_elem, p_face, p_normal, p_count, elem, face, normal, w_trace, w_flux, w_lift, out,
-    step_out, table, total, even, odd, theirs, lifted,
+    step_out, table, total, even, odd, theirs, c_ref, l1_ref, l2_ref, l3_ref, arrived,
 ):
     step = pl.program_id(0)
     last_tile = elem.shape[1] // TILE - 1
@@ -404,12 +426,14 @@
     @pl.when(step == 0)
     def _():
         step_out[0, 0] = tau
-        total[...] = jnp.zeros_like(total)
-        for j in range(c_ref.shape[1] // CHUNK):
-            cols = slice(j * CHUNK, (j + 1) * CHUNK)
-            table[:, cols] = split2_rows(
-                combine(c_ref[:, cols], l1_ref[:, cols], l2_ref[:, cols], half, sixth)
+        loads = [
+            pltpu.make_async_copy(source, target, arrived.at[i])
+            for i, (source, target) in enumerate(
+                ((c_any, c_ref), (l1_any, l1_ref), (l2_any, l2_ref), (l3_any, l3_ref))
             )
+        ]
+        for load in loads:
+            load.start()
         left = lax.broadcasted_iota(jnp.int32, (ROWS, 128), 1) < 64
         theirs[0 : 3 * TROWS, 0:256] = from_lower[...]
         theirs[0 : 3 * TROWS, 256:512] = from_upper[...]
@@ -418,11 +442,21 @@
             one, two = from_peer[2 * m], from_peer[2 * m + 1]
             theirs[0:ROWS, cols] = jnp.where(left, one, pltpu.roll(two, 64, 1))
             theirs[ROWS : 2 * ROWS, cols] = jnp.where(left, pltpu.roll(one, 64, 1), two)
-        slots = lax.broadcasted_iota(jnp.int32, p_elem.shape, 1)
-        alive = jnp.where(slots < p_count[...], 1.0, 0.0)
+        slot = lax.broadcasted_iota(jnp.int32, (1, 128), 1)
+        alive = jnp.concatenate(
+            [
+                jnp.where(
+                    slot < 64,
+                    jnp.where(slot < p_count[0:1, 2 * m : 2 * m + 1], 1.0, 0.0),
+                    jnp.where(slot - 64 < p_count[0:1, 2 * m + 1 : 2 * m + 2], 1.0, 0.0),
+                )
+                for m in range(4)
+            ],
+            axis=1,
+        )
         b_elem = jnp.concatenate([join_slab(s_elem), join_peers(p_elem[...])], axis=1)
         b_face = jnp.concatenate([join_slab(s_face), join_peers(p_face[...])], axis=1)
-        b_live = jnp.concatenate([jnp.ones((1, 512), F32), join_peers(alive)], axis=1)
+        b_live = jnp.concatenate([jnp.ones((1, 512), F32), alive], axis=1)
         b_normal = jnp.concatenate(
             [
                 jnp.concatenate([join_slab(s_normal.at[d]), join_peers(p_normal[d])], axis=1)
@@ -430,7 +464,7 @@
             ],
             axis=0,
         )
-        build_selection(b_elem, odd)
+        build_selection(b_elem, odd.at[:, 0:1024])
         index_row, _ = sides(0)
         build_selection(index_row, even)
 
@@ -441,8 +475,19 @@
 
         central, upwind = flux_parts(merged(own), merged(theirs), b_normal, w_flux)
         values = (0.5 * (central - upwind)) * b_live
-        lifted[...] = lift_values(values, b_face, w_lift)
-        add_selected(lifted[...], odd, total)
+        total[...] = lax.dot_general(
+            lift_values(values, b_face, w_lift),
+            odd[:, 0:1024],
+            (((1,), (1,)), ((), ())),
+            preferred_element_type=F32,
+        )
+        for load in loads:
+            load.wait()
+        for j in range(c_ref.shape[1] // CHUNK):
+            cols = slice(j * CHUNK, (j + 1) * CHUNK)
+            table[:, cols] = split2_rows(
+                combine(c_ref[:, cols], l1_ref[:, cols], l2_ref[:, cols], half, sixth)
+            )
     for parity in range(2):
         tile = 2 * step + parity
         cur, nxt = (even, odd) if parity == 0 else (odd, even)
@@ -470,7 +515,7 @@
     return pl.pallas_call(
         rate_kernel,
         grid=(faces // TILE // 2,),
-        in_specs=[whole] * 22,
+        in_specs=[pl.BlockSpec(memory_space=pl.ANY)] * 4 + [whole] * 18,
         out_specs=(whole, pl.BlockSpec(memory_space=pltpu.SMEM)),
         out_shape=(
             jax.ShapeDtypeStruct((BASIS, VARS, elems), F32),
@@ -482,7 +527,11 @@
             pltpu.VMEM((elems, 2 * TILE), BF16),
             pltpu.VMEM((elems, 2 * TILE), BF16),
             pltpu.VMEM((2 * ROWS, 1024), F32),
-            pltpu.VMEM((2 * ROWS, 2 * TILE), BF16),
+            pltpu.VMEM((ROWS, elems), F32),
+            pltpu.VMEM((ROWS, elems), F32),
+            pltpu.VMEM((ROWS, elems), F32),
+            pltpu.VMEM((ROWS, elems), F32),
+            pltpu.SemaphoreType.DMA((4,)),
         ],
         name="rate",
     )(*fields, geom, own, *received, *border, *inner, *weights)
@@ -531,6 +580,7 @@
             jax.ShapeDtypeStruct((8, elems), F32),
             jax.ShapeDtypeStruct((slabs, 1, 128), F32),
         ),
+        in_specs=[pl.BlockSpec(memory_space=pltpu.VMEM)] * 6 + [pl.BlockSpec(memory_space=pl.ANY)],
         scratch_shapes=[pltpu.VMEM((8, vertex_velocity.shape[1] + 256), F32)],
         name="mesh",
     )(
@@ -540,23 +590,27 @@
         elem_vertex,
         cell_size.reshape(1, elems),
         sound_speed.reshape(1, elems),
+        w_flux,
     )
     slab_least = lax.all_to_all(least, "shock", split_axis=0, concat_axis=0, tiled=True)
 
     state = jnp.transpose(conserved, (1, 0, 2))
     first, second, third, own, slab_down, slab_up, peer_send = make_front(
-        state, geom, slab_least, (slab_elem, slab_face, peer_elem, peer_face), w_elem, w_trace
+        state, geom, (slab_elem, slab_face, peer_elem, peer_face), w_elem, w_trace
     )
     slab_lower = lax.ppermute(slab_up, "shock", up)
     slab_upper = lax.ppermute(slab_down, "shock", down)
+    peer_send = make_stamp(slab_least, peer_send)
     peer_recv = lax.all_to_all(peer_send, "trans", split_axis=0, concat_axis=0, tiled=True)
     fourth = make_third(third, geom, w_elem)
+    in_vmem = lambda value: pltpu.with_memory_space_constraint(value, pltpu.VMEM)
+    slab_lower, slab_upper, peer_recv = in_vmem(slab_lower), in_vmem(slab_upper), in_vmem(peer_recv)
     rate, step_size = make_rate(
         (first, second, third, fourth),
         geom,
         own,
         (slab_lower, slab_upper, peer_recv),
-        (slab_elem, slab_face, slab_normal, peer_elem, peer_face, peer_normal, peer_count),
+        (slab_elem, slab_face, slab_normal, peer_elem, peer_face, peer_normal, peer_count.reshape(1, -1)),
         (inner_elem, inner_face, inner_normal),
         (w_trace, w_flux, w_lift),
     )

time: 104 us -> 94.4 us (0.908)
  the two profiles are of different devices: /device:TPU:14 before, /device:TPU:110 now
where the time goes in v2:
time: 94.4 us; the launch traced here: 93.7 us
  Pallas kernels  55.6 us (59%)
  starting transfers between devices  25.6 us (27%)
  waiting for transfers between devices  10.3 us (11%)
  local copies, waits for them, and re-layouts  1.19 us (1%)
    pallas_call x1, Pallas kernels, make_rate(): pl.pallas_call(rate_kernel, grid=(faces // TILE // 2,), in_specs=[pl.Bloc...  31.9 us
    pallas_call x1, Pallas kernels, make_front(): pl.pallas_call(front_kernel, grid=(chunks + 2,), in_specs=[pl.BlockSpec((...  11.4 us
    all_to_all x1, starting transfers between devices, body(): lax.all_to_all(least, 'shock', split_axis=0, concat_axis=0, tiled=True)  7.37 us
    ppermute x1, waiting for transfers between devices, body(): slab_upper = lax.ppermute(slab_down, 'shock', down)  6.13 us
    ppermute x1, starting transfers between devices, body(): from_lower = lax.ppermute(to_upper, 'shock', up)  4.94 us
    all_to_all x1, starting transfers between devices, body(): lax.all_to_all(peer_send, 'trans', split_axis=0, concat_axis=0, tiled=True)  4.92 us
    ppermute x1, starting transfers between devices, body(): slab_lower = lax.ppermute(slab_up, 'shock', up)  4.57 us
    pallas_call x1, Pallas kernels, make_third(): pl.pallas_call(third_kernel, grid=(elems // CHUNK,), in_specs=[pl.BlockSp...  4.32 us
  transfers between devices with their start and end apart: 6, of which 2 were waited for; matrix products, arithmetic and copies ran while one was open for 0% of the time, Pallas kernels for 20%

profile of v2, /device:TPU:110, one launch (start us, length us, event | category | flops | bytes accessed | tf_op | source)
XLA Modules:
  0.0 93.7 jit_solution(16146800153317981649)
XLA Ops:
  0.6 1.4 %share.2 = (f32[8,128]{1,0:T(8,128)}, f32[8,128]{1,0:T(8,128)}) custom-call(f32[3,512]{1,0:T(4,128)} %velocity.3, s32[2,128]{1,0:T(2,128)} %share.3), custom_call_target="tpu_custom_call" | custom-call | tf_op jit(solution)/shard_map/share/pallas_call | solution.py:568
  2.0 4.9 %collective-permute-start = (f32[8,128]{1,0:T(8,128)}, f32[8,128]{1,0:T(8,128)S(1)}, u32[]{:S(2)}, u32[]{:S(2)}) collective-permute-start(f32[8,128]{1,0:T(8,128)} %get-tuple-element.19), channel_id=1, source_target_pairs={{0,8},{8,16},{16,24},{24,32},{32,40},{40,48},{48,56},{56,64},{64,7... | collective-permute-start | bytes 12296 | tf_op jit(solution)/shard_map/ppermute | solution.py:574
  7.0 1.9 %collective-permute-start.1 = (f32[8,128]{1,0:T(8,128)}, f32[8,128]{1,0:T(8,128)S(1)}, u32[]{:S(2)}, u32[]{:S(2)}) collective-permute-start(f32[8,128]{1,0:T(8,128)} %get-tuple-element.20), channel_id=1, source_target_pairs={{8,0},{16,8},{24,16},{32,24},{40,32},{48,40},{56,48},{64,56},{72,6... | collective-permute-start | bytes 12296 | tf_op jit(solution)/shard_map/ppermute | solution.py:575
  8.9 2.9 %weights.1 = (bf16[448,336]{1,0:T(8,128)(2,1)}, bf16[288,336]{1,0:T(8,128)(2,1)}, bf16[216,216]{1,0:T(8,128)(2,1)}, bf16[448,216]{1,0:T(8,128)(2,1)}) custom-call(f32[11,3,11]{2,1,0:T(4,128)} %bitcast.11, f32[10,3,10]{2,1,0:T(4,128)} %bitcast.12, f32[6,4,10]{2,1,0:T(4,128)} %bitcast.13, f32[6,4,10]{2,1,0:T(4,128)} %bitcast.14, ...), custom_call_target="tpu_custom_call" | custom-call | flops 4000000 | bytes 2000000 | tf_op jit(solution)/shard_map/weights/pallas_call | solution.py:117
  11.8 0.0 collective-permute-done.from_lower
  11.8 0.0 copy-start.1
  11.8 4.2 %collective-permute-done.1.from_upper = f32[8,128]{1,0:T(8,128)S(1)} collective-permute-done((f32[8,128]{1,0:T(8,128)}, f32[8,128]{1,0:T(8,128)S(1)}, u32[]{:S(2)}, u32[]{:S(2)}) %collective-permute-start.1) | collective-permute-done | bytes 4128 | tf_op jit(solution)/shard_map/ppermute | solution.py:575
  16.0 0.0 copy-start.2
  16.0 0.0 copy-done.1
  16.0 0.6 copy-done.2
  16.6 2.2 %mesh.1 = (f32[8,2048]{1,0:T(8,128)}, f32[32,1,128]{2,1,0:T(1,128)}) custom-call(f32[3,512]{1,0:T(4,128)} %velocity.3, f32[8,128]{1,0:T(8,128)} %copy-done.1, f32[8,128]{1,0:T(8,128)} %copy-done.2, s32[4,2048]{1,0:T(4,128)} %corners.1, f32[1,2048]{1,0:T(1,128)} %bitcast.15, f32[1,2048]{1,0:T(1,128)} %bitcast.16, bf16[216,216]{1,0:T(8,128)(2,1)} %get-tuple-element.21.after.w_flux), custom_call_target="tpu_custom_call" | custom-call | tf_op jit(solution)/shard_map/mesh/pallas_call | solution.py:577
  18.8 7.4 %all-to-all-start = ((f32[32,1,128]{2,1,0:T(1,128)}), f32[32,1,128]{2,1,0:T(1,128)S(1)}, u32[]{:S(2)}, u32[]{:S(2)}) async-start(f32[32,1,128]{2,1,0:T(1,128)} %get-tuple-element.31), calls=%async_computation | async-start | bytes 32768 | tf_op jit(solution)/shard_map/all_to_all | solution.py:595
  26.2 11.4 %front.1 = (f32[112,2048]{1,0:T(8,128)}, f32[112,2048]{1,0:T(8,128)}, f32[112,2048]{1,0:T(8,128)}, f32[224,1024]{1,0:T(8,128)}, f32[216,256]{1,0:T(8,128)}, /*index=5*/f32[216,256]{1,0:T(8,128)}, f32[8,112,128]{2,1,0:T(8,128)}) custom-call(f32[10,11,2048]{2,1,0:T(8,128)} %bitcast.10, f32[8,2048]{1,0:T(8,128)} %get-tuple-element.22.geom, s32[2,256]{1,0:T(2,128)} %s_elem.3, ...), custom_call_target="tpu_custom_call" | custom-call | tf_op jit(solution)/shard_map/front/pallas_call | solution.py:332
  37.5 0.0 copy-start.4
  37.5 0.0 copy-start.3
  37.6 0.0 all-to-all-done.least
  37.6 0.0 copy-start
  37.6 0.6 copy-done
  38.2 1.5 %stamp.1 = f32[8,112,128]{2,1,0:T(8,128)} custom-call(f32[32,1,128]{2,1,0:T(1,128)} %copy-done, f32[8,112,128]{2,1,0:T(8,128)} %get-tuple-element.32.value), custom_call_target="tpu_custom_call", output_to_operand_aliasing={{}: (1, {})} | custom-call | tf_op jit(solution)/shard_map/stamp/pallas_call | solution.py:366
  39.7 4.9 %all-to-all-start.1 = ((f32[8,112,128]{2,1,0:T(8,128)}), f32[8,112,128]{2,1,0:T(8,128)S(1)}, u32[]{:S(2)}, u32[]{:S(2)}) async-start(f32[8,112,128]{2,1,0:T(8,128)} %stamp.1), calls=%async_computation.1 | async-start | bytes 917504 | tf_op jit(solution)/shard_map/all_to_all | solution.py:604
  44.6 0.0 copy-done.4
  44.6 4.6 %collective-permute-start.2 = (f32[216,256]{1,0:T(8,128)S(1)}, f32[216,256]{1,0:T(8,128)S(1)}, u32[]{:S(2)}, u32[]{:S(2)}) collective-permute-start(f32[216,256]{1,0:T(8,128)S(1)} %copy-done.4), channel_id=1, source_target_pairs={{0,8},{8,16},{16,24},{24,32},{32,40},{40,48},{48,56},{56,64},{64,7... | collective-permute-start | bytes 663560 | tf_op jit(solution)/shard_map/ppermute | solution.py:601
  49.2 0.0 copy-done.3
  49.2 1.9 %collective-permute-start.3 = (f32[216,256]{1,0:T(8,128)S(1)}, f32[216,256]{1,0:T(8,128)S(1)}, u32[]{:S(2)}, u32[]{:S(2)}) collective-permute-start(f32[216,256]{1,0:T(8,128)S(1)} %copy-done.3), channel_id=1, source_target_pairs={{8,0},{16,8},{24,16},{32,24},{40,32},{48,40},{56,48},{64,56},{72,6... | collective-permute-start | bytes 663560 | tf_op jit(solution)/shard_map/ppermute | solution.py:602
  51.1 4.3 %third.1.l3_any = f32[112,2048]{1,0:T(8,128)} custom-call(f32[112,2048]{1,0:T(8,128)} %get-tuple-element.27.l2_ref.l2_any, f32[8,2048]{1,0:T(8,128)} %get-tuple-element.22.geom, bf16[448,336]{1,0:T(8,128)(2,1)} %get-tuple-element.23.w_elem), custom_call_target="tpu_custom_call" | custom-call | flops 616562688 | bytes 2000000 | tf_op jit(solution)/shard_map/third/pallas_call | solution.py:216
  55.4 0.0 collective-permute-done.2.from_lower
  55.4 6.1 %collective-permute-done.3.from_upper = f32[216,256]{1,0:T(8,128)S(1)} collective-permute-done((f32[216,256]{1,0:T(8,128)S(1)}, f32[216,256]{1,0:T(8,128)S(1)}, u32[]{:S(2)}, u32[]{:S(2)}) %collective-permute-start.3) | collective-permute-done | bytes 221216 | tf_op jit(solution)/shard_map/ppermute | solution.py:602
  61.6 0.0 all-to-all-done.1.from_peer
  61.6 31.9 %rate.1 = (f32[10,11,2048]{2,1,0:T(8,128)}, f32[1,1]{1,0:T(1,128)}) custom-call(f32[112,2048]{1,0:T(8,128)} %get-tuple-element.25.c_any, f32[112,2048]{1,0:T(8,128)} %get-tuple-element.26.l1_any, f32[112,2048]{1,0:T(8,128)} %get-tuple-element.27.l2_ref.l2_any, f32[112,2048]{1,0:T(8,128)} %third.1.l3_any, f32[8,2048]{1,0:T(8,128)} %get-tuple-element.22.geom, ...), custom_call_target="tpu_custom_call" | custom-call | tf_op jit(solution)/shard_map/rate/pallas_call | solution.py:515
Async XLA Ops:
  2.0 9.8 %collective-permute-start = (f32[8,128]{1,0:T(8,128)}, f32[8,128]{1,0:T(8,128)S(1)}, u32[]{:S(2)}, u32[]{:S(2)}) collective-permute-start(f32[8,128]{1,0:T(8,128)} %get-tuple-element.19), channel_id=1, source_target_pairs={{0,8},{8,16},{16,24},{24,32},{32,40},{40,48},{48,56},{56,64},{64,7... | collective-permute-start | bytes 12296 | tf_op jit(solution)/shard_map/ppermute | solution.py:574
  7.0 9.0 %collective-permute-start.1 = (f32[8,128]{1,0:T(8,128)}, f32[8,128]{1,0:T(8,128)S(1)}, u32[]{:S(2)}, u32[]{:S(2)}) collective-permute-start(f32[8,128]{1,0:T(8,128)} %get-tuple-element.20), channel_id=1, source_target_pairs={{8,0},{16,8},{24,16},{32,24},{40,32},{48,40},{56,48},{64,56},{72,6... | collective-permute-start | bytes 12296 | tf_op jit(solution)/shard_map/ppermute | solution.py:575
  11.8 4.2 %copy-start.1 = (f32[8,128]{1,0:T(8,128)}, f32[8,128]{1,0:T(8,128)S(1)}, u32[]{:S(2)}) copy-start(f32[8,128]{1,0:T(8,128)S(1)} %collective-permute-done.from_lower) | copy-start | bytes 12292
  16.0 0.6 copy-start.2
  18.8 18.8 %all-to-all-start = ((f32[32,1,128]{2,1,0:T(1,128)}), f32[32,1,128]{2,1,0:T(1,128)S(1)}, u32[]{:S(2)}, u32[]{:S(2)}) async-start(f32[32,1,128]{2,1,0:T(1,128)} %get-tuple-element.31), calls=%async_computation | async-start | bytes 32768 | tf_op jit(solution)/shard_map/all_to_all | solution.py:595
  37.5 7.1 %copy-start.4 = (f32[216,256]{1,0:T(8,128)S(1)}, f32[216,256]{1,0:T(8,128)}, u32[]{:S(2)}) copy-start(f32[216,256]{1,0:T(8,128)} %get-tuple-element.29) | copy-start | bytes 663556
  37.5 11.6 %copy-start.3 = (f32[216,256]{1,0:T(8,128)S(1)}, f32[216,256]{1,0:T(8,128)}, u32[]{:S(2)}) copy-start(f32[216,256]{1,0:T(8,128)} %get-tuple-element.30) | copy-start | bytes 663556
  37.6 0.6 copy-start
  39.7 21.9 %all-to-all-start.1 = ((f32[8,112,128]{2,1,0:T(8,128)}), f32[8,112,128]{2,1,0:T(8,128)S(1)}, u32[]{:S(2)}, u32[]{:S(2)}) async-start(f32[8,112,128]{2,1,0:T(8,128)} %stamp.1), calls=%async_computation.1 | async-start | bytes 917504 | tf_op jit(solution)/shard_map/all_to_all | solution.py:604
  44.6 10.8 %collective-permute-start.2 = (f32[216,256]{1,0:T(8,128)S(1)}, f32[216,256]{1,0:T(8,128)S(1)}, u32[]{:S(2)}, u32[]{:S(2)}) collective-permute-start(f32[216,256]{1,0:T(8,128)S(1)} %copy-done.4), channel_id=1, source_target_pairs={{0,8},{8,16},{16,24},{24,32},{32,40},{40,48},{48,56},{56,64},{64,7... | collective-permute-start | bytes 663560 | tf_op jit(solution)/shard_map/ppermute | solution.py:601
  49.2 12.4 %collective-permute-start.3 = (f32[216,256]{1,0:T(8,128)S(1)}, f32[216,256]{1,0:T(8,128)S(1)}, u32[]{:S(2)}, u32[]{:S(2)}) collective-permute-start(f32[216,256]{1,0:T(8,128)S(1)} %copy-done.3), channel_id=1, source_target_pairs={{8,0},{16,8},{24,16},{32,24},{40,32},{48,40},{56,48},{64,56},{72,6... | collective-permute-start | bytes 663560 | tf_op jit(solution)/shard_map/ppermute | solution.py:602
